TPU v7x, 32 devices: a whole 2x2x4 slice. The times are simulated.
32 devices in a mesh: grp: 16 (over z, x, core), slab: 2 (over y).
Axes of the slice: x: 2, y: 2, z: 4, core: 2. Of those that a mesh axis runs over, the one named last changes fastest.
Arguments:
- ligand_grids: float32 [2, 4, 128, 128, 128], P(None, None, 'grp', 'slab'), may hold values from -6 to 6
- receptor_kernel: bfloat16 [16, 2, 2, 128, 128, 128], P('grp', None, None, 'slab'), may hold values from -3 to 3
Outputs:
- best_score: bfloat16 [16, 128, 128, 128], P('grp', None, 'slab')
All inputs are finite; a program needn't handle non-finite values.
Results may differ from a plain program's by a relative error of at most 0.018.
Values may be sent and summed in bfloat16 or wider, within the bound.
A program may use at most 128 MiB of HBM per device.

v0:
```python
import math

import jax
import jax.numpy as jnp
from jax import lax
from jax.sharding import PartitionSpec as P

highest = lax.Precision.HIGHEST


def coefficients(length, inverse):
    positions = jnp.arange(length, dtype=jnp.int32)
    phases = positions[:, None] * positions[None, :] % length
    angles = phases.astype(jnp.float32) * (2.0 * math.pi / length)
    scaling = 1.0 / math.sqrt(length)
    cosine = jnp.cos(angles) * scaling
    sine_part = jnp.sin(angles) * scaling
    if inverse:
        sine_part = -sine_part
    upper_rows = jnp.stack([cosine, sine_part])
    lower_rows = jnp.stack([-sine_part, cosine])
    return jnp.stack([upper_rows, lower_rows])


def pack_pairs(ligand_piece):
    stacked = jnp.stack([ligand_piece[:, 0::2], ligand_piece[:, 1::2]])
    return stacked.reshape((2, stacked.shape[1] * stacked.shape[2]) + stacked.shape[3:])


def body(ligand_grids, receptor_kernel):
    length = ligand_grids.shape[4]
    rotations = ligand_grids.shape[0]
    channel_pairs = ligand_grids.shape[1] // 2
    forward = coefficients(length, False)
    forward_low = forward.astype(jnp.bfloat16)
    inverse_low = coefficients(length, True).astype(jnp.bfloat16)
    packed = pack_pairs(ligand_grids)
    lines = jnp.einsum("pqkn,qrzxn->pkrzx", forward, packed, precision=highest)
    columns = lax.all_to_all(
        lines.astype(jnp.bfloat16), "grp", split_axis=1, concat_axis=3, tiled=True
    ).astype(lines.dtype)
    partial_value = jnp.einsum("pqkn,qyrnx->pyrkx", forward, columns, precision=highest).astype(
        jnp.bfloat16
    )
    pieces = jnp.einsum(
        "pqkn,qyrzn->pyrzk",
        forward_low,
        lax.all_to_all(partial_value, "slab", split_axis=3, concat_axis=4, tiled=True),
        preferred_element_type=jnp.float32,
    ).astype(jnp.bfloat16)
    collected = lax.all_gather(pieces, "grp", axis=1, tiled=True)
    spectrum = jnp.transpose(collected, (0, 2, 3, 4, 1))
    spec_split = spectrum.reshape((2, rotations, channel_pairs) + spectrum.shape[2:])
    kernel_one = receptor_kernel[0]
    kernel_real = kernel_one[0][None].astype(jnp.float32)
    kernel_imag = kernel_one[1][None].astype(jnp.float32)
    spec_real = spec_split[0].astype(jnp.float32)
    spec_imag = spec_split[1].astype(jnp.float32)
    real_part = jnp.sum(kernel_real * spec_real - kernel_imag * spec_imag, axis=1)
    imag_part = jnp.sum(kernel_real * spec_imag + kernel_imag * spec_real, axis=1)
    product = jnp.stack([real_part, imag_part]).astype(jnp.bfloat16)
    rows_done = jnp.einsum(
        "pqkn,qrznm->przkm", inverse_low, product, preferred_element_type=jnp.float32
    ).astype(jnp.bfloat16)
    planes = jnp.einsum(
        "pqkn,qrzxn->przxk", inverse_low, rows_done, preferred_element_type=jnp.float32
    ).astype(jnp.bfloat16)
    scores = jnp.einsum(
        "qkn,qrnxy->rkxy",
        inverse_low[0],
        lax.all_to_all(planes, "slab", split_axis=3, concat_axis=2, tiled=True),
        preferred_element_type=jnp.float32,
    )
    return jnp.max(scores, axis=0).astype(jnp.bfloat16)[None]


def solution(mesh):
    return jax.shard_map(
        body,
        mesh=mesh,
        in_specs=(P(None, None, "grp", "slab", None), P("grp", None, None, "slab", None, None)),
        out_specs=P("grp", None, "slab", None),
        check_vma=False,
    )
```

profile of v0, /device:TPU:0, one launch (start us, length us, event | category | flops | bytes accessed | tf_op | source)
XLA Modules:
  0.0 428.9 jit_solution(18179298888462412341)
XLA Ops:
  6.5 0.3 sine_multiply_fusion
  7.1 1.7 fusion.59
  8.8 1.8 bitcast_convert_fusion.6
  10.6 3.0 copy.32
  13.6 1.5 reshape.162
  15.1 31.9 %all_to_all.54 = bf16[16,2,16384]{2,1,0:T(2,128)(2,1)S(1)} all-to-all(bf16[16,2,16384]{2,1,0:T(2,128)(2,1)S(1)} %reshape.162), channel_id=1, replica_groups=mesh['grp'=16,'slab'=2] {'grp'}, dimensions={0} | all-to-all | bytes 2097152 | tf_op jit(solution)/shard_map/all_to_all | solution.py:39
  47.0 1.3 reshape.163
  48.3 3.0 fusion.26
  51.3 4.8 %copy.36 = bf16[2,8,4,128,64]{4,0,2,1,3:T(2,128)(2,1)S(1)} copy(bf16[2,8,4,128,64]{3,4,0,2,1:T(8,128)(2,1)} %fusion.26) | data formatting | bytes 2097152 | tf_op jit(solution)/shard_map/convert_element_type | solution.py:42
  56.1 1.6 reshape.164
  57.8 18.7 %all_to_all.55 = bf16[2,2,131072]{2,1,0:T(2,128)(2,1)} all-to-all(bf16[2,2,131072]{2,1,0:T(2,128)(2,1)S(1)} %reshape.164), channel_id=1, replica_groups=mesh['grp'=16,'slab'=2] {'slab'}, dimensions={0} | all-to-all | bytes 2097152 | tf_op jit(solution)/shard_map/all_to_all | solution.py:48
  76.5 2.6 reshape.165
  79.1 3.5 copy.90
  82.6 3.9 reshape.151
  86.5 0.5 fusion.29
  87.0 1.1 copy.38
  88.1 11.8 %bitcast_convert_fusion.3 = (f32[2,64,128,128]{3,2,1,0:T(8,128)}, f32[2,64,128,128]{3,2,1,0:T(8,128)}) fusion(bf16[1,2,2,64,128,128]{5,4,3,2,1,0:T(8,128)(2,1)} %param.3), kind=kLoop, calls=%fused_computation.25 | loop fusion | flops 4194304 | bytes 25165824 | tf_op jit(solution)/shard_map/convert_element_type | solution.py:55
  99.9 8.7 %copy.31 = f32[2,64,128,128]{2,1,0,3:T(8,128)} copy(f32[2,64,128,128]{3,2,1,0:T(8,128)} %get-tuple-element.9) | data formatting | bytes 16777216 | tf_op jit(solution)/shard_map/convert_element_type | solution.py:55
  108.6 8.8 %copy.39 = f32[2,64,128,128]{2,1,0,3:T(8,128)} copy(f32[2,64,128,128]{3,2,1,0:T(8,128)} %get-tuple-element.10) | data formatting | bytes 16777216 | tf_op jit(solution)/shard_map/convert_element_type | solution.py:56
  117.7 0.3 fusion.48
  118.0 95.6 %all-gather.2.cloned.1.call-done = bf16[2,128,4,64,128]{4,3,2,0,1:T(8,128)(2,1)} async-done(((bf16[2,8,4,64,128]{4,3,2,0,1:T(8,128)(2,1)}), bf16[2,128,4,64,128]{4,3,2,0,1:T(8,128)(2,1)}) %all-gather.2.cloned.1.call-update) | async-done | bytes 16777232 | tf_op jit(solution)/shard_map/all_gather | solution.py:51
  213.5 15.2 %fusion.58 = (bf16[1,4,64,128,128]{3,2,1,0,4:T(8,128)(2,1)}, bf16[1,4,64,128,128]{3,2,1,0,4:T(8,128)(2,1)}) fusion(bf16[2,4,64,128,128]{3,2,1,0,4:T(8,128)(2,1)} %bitcast.146), kind=kLoop, calls=%fused_computation.75 | loop fusion | bytes 33554432 | tf_op jit(solution)/shard_map/slice | solution.py:57
  228.8 17.2 %fusion.1 = (bf16[2,64,128,128]{2,1,0,3:T(8,128)(2,1)}, bf16[2,64,128,128]{2,1,0,3:T(8,128)(2,1)}) fusion(bf16[2,2,64,128,128]{3,2,1,0,4:T(8,128)(2,1)} %bitcast.144, bf16[2,2,64,128,128]{3,2,1,0,4:T(8,128)(2,1)} %bitcast.143, f32[2,64,128,128]{2,1,0,3:T(8,128)} %copy.39, f32[2,64,128,128]{2,1,0,3:T(8,128)S(1)} %copy-done), kind=kLoop, calls=%fused_computation.5 | loop fusion | flops 37748736 | bytes 41943040 | tf_op jit(solution)/shard_map/reduce_sum | solution.py:59
  246.0 7.0 %copy.88 = bf16[2,64,128,128]{2,3,1,0:T(8,128)(2,1)} copy(bf16[2,64,128,128]{2,1,0,3:T(8,128)(2,1)} %get-tuple-element.5) | data formatting | bytes 8388608 | tf_op jit(solution)/shard_map/reduce_sum | solution.py:59
  253.0 4.6 %copy.89 = bf16[2,64,128,128]{2,3,1,0:T(8,128)(2,1)} copy(bf16[2,64,128,128]{2,1,0,3:T(8,128)(2,1)S(1)} %copy-done.1) | data formatting | bytes 8388608 | tf_op jit(solution)/shard_map/reduce_sum | solution.py:60
  257.6 9.3 %fusion.7 = bf16[2,2,64,128,128]{4,3,0,2,1:T(8,128)(2,1)} fusion(bf16[1,2,64,128,128]{3,4,0,2,1:T(8,128)(2,1)} %bitcast.153, bf16[1,2,64,128,128]{3,4,0,2,1:T(8,128)(2,1)} %bitcast.152, bf16[1,2,128,128]{3,2,1,0:T(8,128)(2,1)S(1)} %get-tuple-element.16, bf16[1,2,128,128]{3,2,1,0:T(8,128)(2,1)S(1)} %get-tuple-element.15), kind=kOutput, calls=%fused_computation.12 | convolution fusion | flops 4320657408 | bytes 16908288 | tf_op jit(solution)/shard_map/pqkn,qrzxn->przxk/dot_general | solution.py:65
  266.9 12.2 %copy.43 = bf16[2,2,64,128,128]{4,0,2,1,3:T(2,128)(2,1)S(1)} copy(bf16[2,2,64,128,128]{4,3,0,2,1:T(8,128)(2,1)} %fusion.7) | data formatting | bytes 16777216 | tf_op jit(solution)/shard_map/convert_element_type | solution.py:67
  279.1 97.3 %all_to_all.56 = bf16[2,2,64,128,128]{4,0,2,1,3:T(2,128)(2,1)} all-to-all(bf16[2,2,64,128,128]{4,0,2,1,3:T(2,128)(2,1)S(1)} %copy.43), channel_id=1, replica_groups=mesh['grp'=16,'slab'=2] {'slab'}, dimensions={3} | all-to-all | bytes 16777216 | tf_op jit(solution)/shard_map/all_to_all | solution.py:71
  376.4 12.0 %copy.44 = bf16[2,2,64,128,128]{4,3,2,1,0:T(8,128)(2,1)} copy(bf16[2,2,64,128,128]{4,0,2,1,3:T(2,128)(2,1)} %all_to_all.56) | data formatting | bytes 16777216 | tf_op jit(solution)/shard_map/all_to_all | solution.py:71
  388.4 9.4 %copy.45 = bf16[2,2,2,64,64,128]{5,4,3,2,1,0:T(8,128)(2,1)} copy(bf16[2,2,2,64,64,128]{5,4,2,3,1,0:T(8,128)(2,1)} %bitcast.145) | data formatting | bytes 16777216 | tf_op jit(solution)/shard_map/all_to_all | solution.py:71
  397.8 21.2 %bitcast_reduce_fusion = bf16[64,128,128]{2,1,0:T(8,128)(2,1)S(1)} fusion(bf16[2,2,128,64,128]{4,3,2,1,0:T(8,128)(2,1)} %bitcast.149, bf16[1,128,128]{2,1,0:T(8,128)(2,1)S(1)} %get-tuple-element.20, bf16[1,128,128]{2,1,0:T(8,128)(2,1)S(1)} %fusion.51), kind=kOutput, calls=%fused_computation.17 | convolution fusion | flops 1074823168 | bytes 10551296 | tf_op jit(solution)/shard_map/qkn,qrnxy->rkxy/dot_general | solution.py:68
  419.0 2.8 copy.47
  (10 shorter events, 0.6 us)
Async XLA Ops:
  6.5 207.0 %all-gather.2.cloned.1.call-start = ((), (), s32[]{:S(2)}) async-start(), calls=%async_computation.3 | async-start | bytes 17825792 | tf_op jit(solution)/shard_map/all_gather | solution.py:51
  213.5 15.2 %copy-start = (f32[2,64,128,128]{2,1,0,3:T(8,128)S(1)}, f32[2,64,128,128]{2,1,0,3:T(8,128)}, u32[]{:S(2)}) copy-start(f32[2,64,128,128]{2,1,0,3:T(8,128)} %copy.31) | copy-start | bytes 25165828
  246.0 7.0 %copy-start.1 = (bf16[2,64,128,128]{2,1,0,3:T(8,128)(2,1)S(1)}, bf16[2,64,128,128]{2,1,0,3:T(8,128)(2,1)}, u32[]{:S(2)}) copy-start(bf16[2,64,128,128]{2,1,0,3:T(8,128)(2,1)} %get-tuple-element.6) | copy-start | bytes 12582916
Sparse Core Ops, SparseCore 0:
  88.2 125.2 all-gather.1
where the time goes:
time: 436 us; the launch traced here: 429 us
  blocking collectives  148 us (34%)
  local copies, waits for them, and re-layouts  106 us (24%)
  waiting for transfers between devices  95.6 us (22%)
  matrix products  35.8 us (8%)
  other arithmetic  30.1 us (7%)
  between operations  13.7 us (3%)
    all_to_all x1, blocking collectives, body(): lax.all_to_all(planes, 'slab', split_axis=3, concat_axis=2, tiled=True)  97.3 us
    all_gather x1, waiting for transfers between devices, body(): collected = lax.all_gather(pieces, 'grp', axis=1, tiled=True)  95.6 us
    all_to_all x1, blocking collectives, body(): lax.all_to_all(lines.astype(jnp.bfloat16), 'grp', split_axis=1, concat_ax...  31.9 us
    all_to_all x2, local copies, waits for them, and re-layouts, body(): lax.all_to_all(planes, 'slab', split_axis=3, concat_axis=2, tiled=True)  21.4 us
    dot_general x1, matrix products, body(): jnp.einsum('qkn,qrnxy->rkxy', inverse_low[0], lax.all_to_all(planes, 'sla...  21.2 us
    all_to_all x1, blocking collectives, body(): lax.all_to_all(partial_value, 'slab', split_axis=3, concat_axis=4, tiled=...  18.7 us
    reduce_sum x1, other arithmetic, body(): jnp.sum(kernel_real * spec_real - kernel_imag * spec_imag, axis=1)  17.2 us
    slice x1, local copies, waits for them, and re-layouts, body(): spec_real = spec_split[0].astype(jnp.float32)  15.2 us
  transfers between devices with their start and end apart: 1, of which 1 were waited for; matrix products, arithmetic and copies ran while one was open for 7% of the time, Pallas kernels for 0%

commit v1 on v0

--- a/solution.py
+++ b/solution.py
@@ -1,8 +1,13 @@
 import math
+
+import functools
 
 import jax
 import jax.numpy as jnp
+import numpy as np
 from jax import lax
+from jax.experimental import pallas as pl
+from jax.experimental.pallas import tpu as pltpu
 from jax.sharding import PartitionSpec as P
 
 highest = lax.Precision.HIGHEST
@@ -74,9 +79,255 @@
     return jnp.max(scores, axis=0).astype(jnp.bfloat16)[None]
 
 
+TILE = 16
+SUB = 8
+f32 = jnp.float32
+bf16 = jnp.bfloat16
+
+
+def waves(length):
+    positions = np.arange(length)
+    angles = (positions[:, None] * positions[None, :] % length) * (2.0 * math.pi / length)
+    scaling = 1.0 / math.sqrt(length)
+    cosine, sine = np.cos(angles) * scaling, np.sin(angles) * scaling
+    forward = np.stack([np.stack([cosine, sine]), np.stack([-sine, cosine])])
+    inverse = np.stack([np.stack([cosine, -sine]), np.stack([sine, cosine])])
+    return forward, inverse
+
+
+def matrices(length, groups):
+    forward, inverse = waves(length)
+    half, side = length // 2, 2 * length
+    block = half // groups
+    fz, fx, ix, mz = [], [], [], []
+    for own in range(2):
+        order = (np.arange(length) + own * half) % length
+        by_cell = forward[:, :, order].reshape(2, 2, length, groups, length // groups)
+        fz.append(by_cell.transpose(0, 2, 3, 1, 4).reshape(side, side))
+        cells = forward[:, :, :, order].reshape(2, 2, length, 2, groups, block)
+        fx.append(cells.transpose(0, 2, 4, 3, 1, 5).reshape(side, side))
+        ix.append(inverse[:, :, order].transpose(0, 2, 1, 3).reshape(side, side))
+        lines = inverse[0][:, :, order].reshape(2, length, length // SUB, SUB)
+        mz.append(lines.transpose(1, 2, 0, 3).reshape(length, side))
+    fy = forward.transpose(1, 3, 0, 2).reshape(side, side)
+    iy = inverse.transpose(1, 3, 0, 2).reshape(side, side)
+    return [np.stack(m).astype(np.float32) for m in (fz, fx, ix, mz)] + [
+        fy.astype(np.float32),
+        iy.astype(np.float32),
+    ]
+
+
+def dot(a, b):
+    return jnp.dot(a, b, preferred_element_type=f32)
+
+
+def split_kernel(rotations, pairs, depth, width, block, lig_ref, out_ref):
+    @pl.loop(0, width)
+    def _(x):
+        for r in range(rotations):
+            for j in range(pairs):
+                parts = []
+                for q in range(2):
+                    first = ((r * pairs + j) * 2 + q) * depth * width
+                    parts.append(lig_ref[pl.ds(first + x, depth, stride=width), :])
+                out_ref[x // block, x % block, r * pairs + j] = jnp.concatenate(parts, 0).astype(bf16)
+
+
+def zy_kernel(rotations, groups, block, length, fz_ref, fy_ref, in_ref, mine_ref, other_ref, hold):
+    fz = fz_ref[...]
+    fy = fy_ref[...]
+    grids = 2 * rotations
+
+    @pl.loop(0, block)
+    def _(x):
+        for r in range(rotations):
+            cols = [
+                jnp.concatenate([in_ref[g, x, 2 * r + j] for g in range(groups)], 0) for j in range(2)
+            ]
+            lines = dot(fz, jnp.concatenate(cols, 1)).astype(bf16)
+            rows = []
+            for j in range(2):
+                at = slice(j * length, (j + 1) * length)
+                rows.append(jnp.concatenate([lines[:length, at], lines[length:, at]], 1))
+            plane = dot(jnp.concatenate(rows, 0), fy)
+            for p in range(2):
+                start = ((p * block + x) * grids + 2 * r) * length
+                hold[pl.ds(start, 2 * length), :] = plane[:, p * length : (p + 1) * length]
+
+    stride = grids * length
+    half = length // 2
+
+    @pl.loop(0, half, unroll=2)
+    def _(k):
+        for i in range(grids):
+            mine_ref[k, i] = hold[pl.ds(i * length + k, 2 * block, stride=stride), :].astype(bf16)
+            other_ref[k, i] = hold[pl.ds(i * length + half + k, 2 * block, stride=stride), :].astype(
+                bf16
+            )
+
+
+def score_kernel(rotations, groups, length, fx_ref, ix_ref, iy_ref, rec_ref, in_ref, mine_ref, other_ref, hold):
+    fx = fx_ref[...]
+    ix = ix_ref[...]
+    iy = iy_ref[...]
+    rows = rotations * length
+
+    @pl.loop(0, SUB, unroll=2)
+    def _(k):
+        kr = [rec_ref[0, j, k].astype(f32) for j in range(2)]
+        ki = [rec_ref[1, j, k].astype(f32) for j in range(2)]
+        real, imag = [], []
+        for r in range(rotations):
+            cols = [
+                jnp.concatenate([in_ref[g, k, 2 * r + j] for g in range(groups)], 0) for j in range(2)
+            ]
+            spec = dot(fx, jnp.concatenate(cols, 1))
+            sr = [spec[:length, j * length : (j + 1) * length] for j in range(2)]
+            si = [spec[length:, j * length : (j + 1) * length] for j in range(2)]
+            real.append(kr[0] * sr[0] - ki[0] * si[0] + (kr[1] * sr[1] - ki[1] * si[1]))
+            imag.append(kr[0] * si[0] + ki[0] * sr[0] + (kr[1] * si[1] + ki[1] * sr[1]))
+        product = jnp.concatenate(
+            [jnp.concatenate(real, 1).astype(bf16), jnp.concatenate(imag, 1).astype(bf16)], 0
+        )
+        done = dot(ix, product).astype(bf16)
+        flat = []
+        for r in range(rotations):
+            at = slice(r * length, (r + 1) * length)
+            flat.append(jnp.concatenate([done[:length, at], done[length:, at]], 1))
+        planes = dot(jnp.concatenate(flat, 0), iy)
+        for p in range(2):
+            hold[p, pl.ds(k * rows, rows), :] = planes[:, p * length : (p + 1) * length]
+
+    half = length // 2
+
+    @pl.loop(0, half, unroll=4)
+    def _(x):
+        for r in range(rotations):
+            for ref, first in ((mine_ref, 0), (other_ref, half)):
+                at = pl.ds(r * length + first + x, SUB, stride=rows)
+                ref[r, x, 0] = jnp.concatenate([hold[0, at, :], hold[1, at, :]], 0).astype(bf16)
+
+
+def last_kernel(rotations, count, length, wide, mz_ref, *refs):
+    ins, out_ref, hold = refs[: 2 * count], refs[-2], refs[-1]
+    mz = mz_ref[...]
+
+    @pl.loop(0, wide, unroll=2)
+    def _(x):
+        cols = []
+        for r in range(rotations):
+            tiles = []
+            for ref in ins:
+                tiles += [ref[r, x, t] for t in range(ref.shape[2])]
+            cols.append(jnp.concatenate(tiles, 0))
+        scores = dot(mz, jnp.concatenate(cols, 1))
+        best = scores[:, :length]
+        for r in range(1, rotations):
+            best = jnp.maximum(best, scores[:, r * length : (r + 1) * length])
+        hold[pl.ds(x * length, length), :] = best
+
+    @pl.loop(0, length, unroll=4)
+    def _(z):
+        out_ref[z] = hold[pl.ds(z, wide, stride=length), :].astype(bf16)
+
+
+CHUNKS = 4
+
+
+def quick_body(groups, ligand_grids, receptor_kernel):
+    rotations, channels, depth, width, length = ligand_grids.shape
+    pairs = channels // 2
+    grids = rotations * pairs
+    half = length // 2
+    block = width // groups
+    side = 2 * length
+    consts = matrices(length, groups)
+    own = lax.axis_index("slab")
+    fz, fx, ix, mz = [
+        lax.dynamic_index_in_dim(jnp.asarray(m).astype(bf16), own, 0, keepdims=False) for m in consts[:4]
+    ]
+    fy, iy = [jnp.asarray(m).astype(bf16) for m in consts[4:]]
+    whole = pl.BlockSpec(memory_space=pltpu.VMEM)
+
+    blocks = pl.pallas_call(
+        functools.partial(split_kernel, rotations, pairs, depth, width, block),
+        out_shape=jax.ShapeDtypeStruct((groups, block, grids, 2 * depth, length), bf16),
+        in_specs=[whole],
+        out_specs=whole,
+    )(ligand_grids.reshape(-1, length))
+    lines = lax.all_to_all(blocks, "grp", split_axis=0, concat_axis=0, tiled=True)
+    shape = jax.ShapeDtypeStruct((half, grids, 2 * block, length), bf16)
+    mine, other = pl.pallas_call(
+        functools.partial(zy_kernel, rotations, groups, block, length),
+        out_shape=[shape, shape],
+        in_specs=[whole] * 3,
+        out_specs=[whole] * 2,
+        scratch_shapes=[pltpu.VMEM((2 * block * grids * length, length), f32)],
+    )(fz, fy, lines)
+    swap = [(0, 1), (1, 0)]
+    came = lax.ppermute(other, "slab", swap)
+    joined = jnp.concatenate([mine, came], axis=2)
+
+    rec = receptor_kernel[0]
+    chunk = half // CHUNKS
+    steps = chunk // SUB
+    own_parts, far_parts = [], []
+    for c in range(CHUNKS):
+        gathered = lax.all_gather(joined[c * chunk : (c + 1) * chunk], "grp", axis=0, tiled=False)
+        part = jax.ShapeDtypeStruct((rotations, half, steps, TILE, length), bf16)
+        keep, send = pl.pallas_call(
+            functools.partial(score_kernel, rotations, groups, length),
+            grid=(steps,),
+            out_shape=[part, part],
+            in_specs=[
+                pl.BlockSpec((side, side), lambda t: (0, 0)),
+                pl.BlockSpec((side, side), lambda t: (0, 0)),
+                pl.BlockSpec((side, side), lambda t: (0, 0)),
+                pl.BlockSpec((2, pairs, SUB, length, length), lambda t, c=c: (0, 0, c * steps + t, 0, 0)),
+                pl.BlockSpec((groups, SUB, grids, TILE, length), lambda t: (0, t, 0, 0, 0)),
+            ],
+            out_specs=[pl.BlockSpec((rotations, half, 1, TILE, length), lambda t: (0, 0, t, 0, 0))] * 2,
+            scratch_shapes=[pltpu.VMEM((2, SUB * rotations * length, length), f32)],
+            cost_estimate=pl.CostEstimate(
+                flops=chunk * 4 * 2 * side**3, bytes_accessed=10 * 2**20, transcendentals=0
+            ),
+        )(fx, ix, iy, rec, gathered)
+        own_parts.append(keep)
+        far_parts.append(lax.ppermute(send, "slab", swap))
+
+    wide = TILE
+    best = pl.pallas_call(
+        functools.partial(last_kernel, rotations, CHUNKS, length, wide),
+        grid=(half // wide,),
+        out_shape=jax.ShapeDtypeStruct((length, half, length), bf16),
+        in_specs=[pl.BlockSpec((length, side), lambda t: (0, 0))]
+        + [pl.BlockSpec((rotations, wide, steps, TILE, length), lambda t: (0, t, 0, 0, 0))] * (2 * CHUNKS),
+        out_specs=pl.BlockSpec((length, wide, length), lambda t: (0, t, 0)),
+        scratch_shapes=[pltpu.VMEM((wide * length, length), f32)],
+    )(mz, *own_parts, *far_parts)
+    return best[None]
+
+
+def choose(groups, slabs, ligand_grids, receptor_kernel):
+    rotations, channels, depth, width, length = ligand_grids.shape
+    fits = (
+        slabs == 2
+        and channels == 4
+        and rotations == 2
+        and depth == SUB
+        and width % groups == 0
+        and 4 * (width // groups) == TILE
+        and length % 128 == 0
+        and (length // 2) % (CHUNKS * SUB) == 0
+    )
+    if fits:
+        return quick_body(groups, ligand_grids, receptor_kernel)
+    return body(ligand_grids, receptor_kernel)
+
+
 def solution(mesh):
     return jax.shard_map(
-        body,
+        functools.partial(choose, mesh.shape["grp"], mesh.shape["slab"]),
         mesh=mesh,
         in_specs=(P(None, None, "grp", "slab", None), P("grp", None, None, "slab", None, None)),
         out_specs=P("grp", None, "slab", None),

time: 436 us -> 329 us (0.75); the launches traced: 429 us -> 329 us
  blocking collectives: 148 us -> 0 us
  waiting for transfers between devices: 95.6 us -> 215 us
  local copies, waits for them, and re-layouts: 106 us -> 5.38 us
  Pallas kernels: 0 us -> 80.5 us
  matrix products: 35.8 us -> 0 us
  other arithmetic: 30.1 us -> 0 us
  starting transfers between devices: 0.01 us -> 15.1 us
    all_to_all x3 -> x0, blocking collectives: 148 us -> none  [the longest x1 97.3 us: body(): lax.all_to_all(planes, 'slab', split_axis=3, concat_axis=2, tiled=True)]
    pallas_call x0 -> x7, Pallas kernels: none -> 80.5 us  [the longest x4 57.6 us: quick_body(): pl.pallas_call(functools.partial(score_kernel, rotations, groups, length)...]
    all_gather x1 -> x4, waiting for transfers between devices: 95.6 us -> 155 us  [quick_body(): lax.all_gather(joined[c * chunk:(c + 1) * chunk], 'grp', axis=0, tiled=Fa...]
    convert_element_type x6 -> x0, local copies, waits for them, and re-layouts: 38.6 us -> none  [the longest x1 12.2 us: body(): planes = jnp.einsum('pqkn,qrzxn->przxk', inverse_low, rows_done, preferre...]
    dot_general x5 -> x0, matrix products: 35.8 us -> none  [the longest x1 21.2 us: body(): jnp.einsum('qkn,qrnxy->rkxy', inverse_low[0], lax.all_to_all(planes, 'sla...]
    ppermute x0 -> x5, waiting for transfers between devices: none -> 35.5 us  [the longest x4 23.5 us: quick_body(): far_parts.append(lax.ppermute(send, 'slab', swap))]
    all_to_all x4 -> x0, local copies, waits for them, and re-layouts: 28.8 us -> none  [the longest x2 21.4 us: body(): lax.all_to_all(planes, 'slab', split_axis=3, concat_axis=2, tiled=True)]
    all_to_all x0 -> x1, waiting for transfers between devices: none -> 22.2 us  [quick_body(): lax.all_to_all(blocks, 'grp', split_axis=0, concat_axis=0, tiled=True)]
  transfers between devices with their start and end apart: 1 -> 10, of which waited for: 1 -> 7; matrix products, arithmetic and copies ran while one was open for 7% -> 1% of each run, Pallas kernels for 0% -> 17%
where the time goes in v1:
time: 329 us
  waiting for transfers between devices  215 us (65%)
  Pallas kernels  80.5 us (24%)
  starting transfers between devices  15.1 us (5%)
  between operations  13.2 us (4%)
  local copies, waits for them, and re-layouts  5.38 us (2%)
    all_gather x4, waiting for transfers between devices, quick_body(): lax.all_gather(joined[c * chunk:(c + 1) * chunk], 'grp', axis=0, tiled=Fa...  155 us
    pallas_call x4, Pallas kernels, quick_body(): pl.pallas_call(functools.partial(score_kernel, rotations, groups, length)...  57.6 us
    ppermute x4, waiting for transfers between devices, quick_body(): far_parts.append(lax.ppermute(send, 'slab', swap))  23.5 us
    all_to_all x1, waiting for transfers between devices, quick_body(): lax.all_to_all(blocks, 'grp', split_axis=0, concat_axis=0, tiled=True)  22.2 us
    ppermute x1, waiting for transfers between devices, quick_body(): came = lax.ppermute(other, 'slab', swap)  12 us
    pallas_call x1, Pallas kernels, quick_body(): pl.pallas_call(functools.partial(last_kernel, rotations, CHUNKS, length,...  11.9 us
    all_to_all x1, starting transfers between devices, quick_body(): lax.all_to_all(blocks, 'grp', split_axis=0, concat_axis=0, tiled=True)  7.52 us
  transfers between devices with their start and end apart: 10, of which 7 were waited for; matrix products, arithmetic and copies ran while one was open for 1% of the time, Pallas kernels for 17%

profile of v1, /device:TPU:0, one launch (start us, length us, event | category | flops | bytes accessed | tf_op | source)
XLA Modules:
  0.0 329.0 jit_solution(11890803454539403473)
XLA Ops:
  6.5 5.1 %shard_map.82 = bf16[16,4,4,16,128]{4,3,2,1,0:T(8,128)(2,1)} custom-call(f32[4096,128]{1,0:T(8,128)} %bitcast.23), custom_call_target="tpu_custom_call" | custom-call | tf_op jit(solution)/shard_map/pallas_call | solution.py:252
  11.6 7.5 %all-to-all-start = ((bf16[16,4,4,16,128]{4,3,2,1,0:T(8,128)(2,1)}), bf16[16,4,4,16,128]{4,3,2,1,0:T(8,128)(2,1)S(1)}, u32[]{:S(2)}, u32[]{:S(2)}) async-start(bf16[16,4,4,16,128]{4,3,2,1,0:T(8,128)(2,1)} %shard_map.82), calls=%async_computation | async-start | bytes 2097152 | tf_op jit(solution)/shard_map/all_to_all | solution.py:258
  19.1 0.0 all-gather.11.cloned.1.call-start
  19.2 0.7 dynamic-slice_bitcast_fusion.fz_ref
  19.9 22.2 %all-to-all-done.in_ref = bf16[16,4,4,16,128]{4,3,2,1,0:T(8,128)(2,1)S(1)} async-done(((bf16[16,4,4,16,128]{4,3,2,1,0:T(8,128)(2,1)}), bf16[16,4,4,16,128]{4,3,2,1,0:T(8,128)(2,1)S(1)}, u32[]{:S(2)}, u32[]{:S(2)}) %all-to-all-start) | async-done | bytes 1048608 | tf_op jit(solution)/shard_map/all_to_all | solution.py:258
  42.0 1.0 copy-done
  43.0 6.0 %shard_map.83 = (bf16[64,4,8,128]{3,2,1,0:T(8,128)(2,1)}, bf16[64,4,8,128]{3,2,1,0:T(8,128)(2,1)}) custom-call(bf16[256,256]{1,0:T(8,128)(2,1)} %dynamic-slice_bitcast_fusion.fz_ref, bf16[256,256]{1,0:T(8,128)(2,1)} %constant.43.fy_ref, bf16[16,4,4,16,128]{4,3,2,1,0:T(8,128)(2,1)} %copy-done), custom_call_target="tpu_custom_call" | custom-call | tf_op jit(solution)/shard_map/pallas_call | solution.py:260
  49.0 1.5 collective-permute-start
  50.5 1.2 constant_dynamic-update-slice_fusion.1
  51.7 12.0 %collective-permute-done = bf16[64,4,8,128]{3,2,1,0:T(8,128)(2,1)S(1)} collective-permute-done((bf16[64,4,8,128]{3,2,1,0:T(8,128)(2,1)}, bf16[64,4,8,128]{3,2,1,0:T(8,128)(2,1)S(1)}, u32[]{:S(2)}, u32[]{:S(2)}) %collective-permute-start) | collective-permute-done | bytes 524320 | tf_op jit(solution)/shard_map/ppermute | solution.py:268
  63.7 0.1 constant_dynamic-update-slice_fusion
  63.9 1.1 fusion
  65.0 0.0 all-gather.13.cloned.1.call-start
  65.0 0.7 all-gather.13.cloned.1.call-update
  65.8 0.7 all-gather.15.cloned.1.call-update
  66.5 0.5 all-gather.9.cloned.1.call-update
  67.0 0.7 dynamic-slice_bitcast_fusion.1
  67.8 49.5 %all-gather.11.cloned.1.call-done = bf16[256,4,16,128]{3,2,1,0:T(8,128)(2,1)} async-done(((bf16[16,4,16,128]{3,2,1,0:T(8,128)(2,1)}), bf16[256,4,16,128]{3,2,1,0:T(8,128)(2,1)}) %all-gather.11.cloned.1.call-update) | async-done | bytes 4194320 | tf_op jit(solution)/shard_map/all_gather | solution.py:276
  117.3 14.4 %shard_map.85 = (bf16[2,64,2,16,128]{4,3,2,1,0:T(8,128)(2,1)}, bf16[2,64,2,16,128]{4,3,2,1,0:T(8,128)(2,1)}) custom-call(bf16[256,256]{1,0:T(8,128)(2,1)} %get-tuple-element.30.fx_ref, bf16[256,256]{1,0:T(8,128)(2,1)} %get-tuple-element.29.ix_ref, bf16[256,256]{1,0:T(8,128)(2,1)} %constant.41.iy_ref, bf16[2,2,64,128,128]{4,3,2,1,0:T(8,128)(2,1)} %bitcast.15, ...), custom_call_target="tpu_custom_call" | custom-call | flops 2147483648 | bytes 10485760 | tf_op jit(solution)/shard_map/pallas_call | solution.py:278
  131.7 1.5 collective-permute-start.2
  133.2 35.2 %all-gather.13.cloned.1.call-done = bf16[256,4,16,128]{3,2,1,0:T(8,128)(2,1)} async-done(((bf16[16,4,16,128]{3,2,1,0:T(8,128)(2,1)}), bf16[256,4,16,128]{3,2,1,0:T(8,128)(2,1)}) %all-gather.13.cloned.1.call-update) | async-done | bytes 4194320 | tf_op jit(solution)/shard_map/all_gather | solution.py:276
  168.4 14.4 %shard_map.86 = (bf16[2,64,2,16,128]{4,3,2,1,0:T(8,128)(2,1)}, bf16[2,64,2,16,128]{4,3,2,1,0:T(8,128)(2,1)}) custom-call(bf16[256,256]{1,0:T(8,128)(2,1)} %get-tuple-element.30.fx_ref, bf16[256,256]{1,0:T(8,128)(2,1)} %get-tuple-element.29.ix_ref, bf16[256,256]{1,0:T(8,128)(2,1)} %constant.41.iy_ref, bf16[2,2,64,128,128]{4,3,2,1,0:T(8,128)(2,1)} %bitcast.16, ...), custom_call_target="tpu_custom_call" | custom-call | flops 2147483648 | bytes 10485760 | tf_op jit(solution)/shard_map/pallas_call | solution.py:278
  182.8 1.5 collective-permute-start.3
  184.3 35.4 %all-gather.15.cloned.1.call-done = bf16[256,4,16,128]{3,2,1,0:T(8,128)(2,1)} async-done(((bf16[16,4,16,128]{3,2,1,0:T(8,128)(2,1)}), bf16[256,4,16,128]{3,2,1,0:T(8,128)(2,1)}) %all-gather.15.cloned.1.call-update) | async-done | bytes 4194320 | tf_op jit(solution)/shard_map/all_gather | solution.py:276
  219.6 14.4 %shard_map.87 = (bf16[2,64,2,16,128]{4,3,2,1,0:T(8,128)(2,1)}, bf16[2,64,2,16,128]{4,3,2,1,0:T(8,128)(2,1)}) custom-call(bf16[256,256]{1,0:T(8,128)(2,1)} %get-tuple-element.30.fx_ref, bf16[256,256]{1,0:T(8,128)(2,1)} %get-tuple-element.29.ix_ref, bf16[256,256]{1,0:T(8,128)(2,1)} %constant.41.iy_ref, bf16[2,2,64,128,128]{4,3,2,1,0:T(8,128)(2,1)} %bitcast.17, ...), custom_call_target="tpu_custom_call" | custom-call | flops 2147483648 | bytes 10485760 | tf_op jit(solution)/shard_map/pallas_call | solution.py:278
  234.0 1.5 collective-permute-start.4
  235.5 35.1 %all-gather.9.cloned.1.call-done = bf16[256,4,16,128]{3,2,1,0:T(8,128)(2,1)} async-done(((bf16[16,4,16,128]{3,2,1,0:T(8,128)(2,1)}), bf16[256,4,16,128]{3,2,1,0:T(8,128)(2,1)}) %all-gather.9.cloned.1.call-update) | async-done | bytes 4194320 | tf_op jit(solution)/shard_map/all_gather | solution.py:276
  270.6 14.4 %shard_map.84 = (bf16[2,64,2,16,128]{4,3,2,1,0:T(8,128)(2,1)}, bf16[2,64,2,16,128]{4,3,2,1,0:T(8,128)(2,1)}) custom-call(bf16[256,256]{1,0:T(8,128)(2,1)} %get-tuple-element.30.fx_ref, bf16[256,256]{1,0:T(8,128)(2,1)} %get-tuple-element.29.ix_ref, bf16[256,256]{1,0:T(8,128)(2,1)} %constant.41.iy_ref, bf16[2,2,64,128,128]{4,3,2,1,0:T(8,128)(2,1)} %bitcast.18, ...), custom_call_target="tpu_custom_call" | custom-call | flops 2147483648 | bytes 10485760 | tf_op jit(solution)/shard_map/pallas_call | solution.py:278
  284.9 1.5 collective-permute-start.1
  286.4 0.6 dynamic-slice_bitcast_fusion.3.mz_ref
  287.1 23.5 %collective-permute-done.1.refs_4_ = bf16[2,64,2,16,128]{4,3,2,1,0:T(8,128)(2,1)} collective-permute-done((bf16[2,64,2,16,128]{4,3,2,1,0:T(8,128)(2,1)}, bf16[2,64,2,16,128]{4,3,2,1,0:T(8,128)(2,1)}, u32[]{:S(2)}, u32[]{:S(2)}) %collective-permute-start.1) | collective-permute-done | bytes 1048608 | tf_op jit(solution)/shard_map/ppermute | solution.py:296
  310.6 11.9 %shard_map.88 = bf16[128,64,128]{2,1,0:T(8,128)(2,1)} custom-call(bf16[128,256]{1,0:T(8,128)(2,1)} %dynamic-slice_bitcast_fusion.3.mz_ref, bf16[2,64,2,16,128]{4,3,2,1,0:T(8,128)(2,1)} %get-tuple-element.17.refs_0_, bf16[2,64,2,16,128]{4,3,2,1,0:T(8,128)(2,1)} %get-tuple-element.18.refs_1_, bf16[2,64,2,16,128]{4,3,2,1,0:T(8,128)(2,1)} %get-tuple-element.19.refs_2_, ...), custom_call_target="tpu_custom_call" | custom-call | tf_op jit(solution)/shard_map/pallas_call | solution.py:299
  (21 shorter events, 0.1 us)
Async XLA Ops:
  6.5 12.6 %copy-start.6 = (bf16[2,256,256]{2,1,0:T(8,128)(2,1)S(1)}, bf16[2,256,256]{2,1,0:T(8,128)(2,1)}, u32[]{:S(2)}) copy-start(bf16[2,256,256]{2,1,0:T(8,128)(2,1)} %constant.42) | copy-start | bytes 786436
  11.6 55.4 %copy-start.4 = (bf16[2,256,256]{2,1,0:T(8,128)(2,1)S(1)}, bf16[2,256,256]{2,1,0:T(8,128)(2,1)}, u32[]{:S(2)}) copy-start(bf16[2,256,256]{2,1,0:T(8,128)(2,1)} %constant.39) | copy-start | bytes 786436
  11.6 55.4 %copy-start.5 = (bf16[2,256,256]{2,1,0:T(8,128)(2,1)S(1)}, bf16[2,256,256]{2,1,0:T(8,128)(2,1)}, u32[]{:S(2)}) copy-start(bf16[2,256,256]{2,1,0:T(8,128)(2,1)} %constant.40) | copy-start | bytes 786436
  11.6 30.4 %all-to-all-start = ((bf16[16,4,4,16,128]{4,3,2,1,0:T(8,128)(2,1)}), bf16[16,4,4,16,128]{4,3,2,1,0:T(8,128)(2,1)S(1)}, u32[]{:S(2)}, u32[]{:S(2)}) async-start(bf16[16,4,4,16,128]{4,3,2,1,0:T(8,128)(2,1)} %shard_map.82), calls=%async_computation | async-start | bytes 2097152 | tf_op jit(solution)/shard_map/all_to_all | solution.py:258
  19.1 98.2 %all-gather.11.cloned.1.call-start = ((), (), s32[]{:S(2)}) async-start(), calls=%async_computation.2 | async-start | bytes 4456448 | tf_op jit(solution)/shard_map/all_gather | solution.py:276
  42.0 1.0 copy-start
  49.0 14.7 %collective-permute-start = (bf16[64,4,8,128]{3,2,1,0:T(8,128)(2,1)}, bf16[64,4,8,128]{3,2,1,0:T(8,128)(2,1)S(1)}, u32[]{:S(2)}, u32[]{:S(2)}) collective-permute-start(bf16[64,4,8,128]{3,2,1,0:T(8,128)(2,1)} %get-tuple-element.16), channel_id=1, source_target_pairs={{0,1},{1,0},{2,3},{3,2},{4,5},{5,4},{6,7},{7,6},{8,9},{9,8},{10,11... | collective-permute-start | bytes 1572872 | tf_op jit(solution)/shard_map/ppermute | solution.py:268
  65.0 103.4 %all-gather.13.cloned.1.call-start = ((), (), s32[]{:S(2)}) async-start(), calls=%async_computation.3 | async-start | bytes 4456448 | tf_op jit(solution)/shard_map/all_gather | solution.py:276
  65.7 153.9 %all-gather.15.cloned.1.call-start = ((), (), s32[]{:S(2)}) async-start(), calls=%async_computation.4 | async-start | bytes 4456448 | tf_op jit(solution)/shard_map/all_gather | solution.py:276
  66.4 204.1 %all-gather.9.cloned.1.call-start = ((), (), s32[]{:S(2)}) async-start(), calls=%async_computation.1 | async-start | bytes 4456448 | tf_op jit(solution)/shard_map/all_gather | solution.py:276
  131.7 155.4 %collective-permute-start.2 = (bf16[2,64,2,16,128]{4,3,2,1,0:T(8,128)(2,1)}, bf16[2,64,2,16,128]{4,3,2,1,0:T(8,128)(2,1)S(1)}, u32[]{:S(2)}, u32[]{:S(2)}) collective-permute-start(bf16[2,64,2,16,128]{4,3,2,1,0:T(8,128)(2,1)} %get-tuple-element.22), channel_id=1, source_target_pairs={{0,1},{1,0},{2,3},{3,2},{4,5},{5,4},{6,7},{7,6},{8,9},{9,8},{10,11... | collective-permute-start | bytes 3145736 | tf_op jit(solution)/shard_map/ppermute | solution.py:296
  182.8 104.3 %collective-permute-start.3 = (bf16[2,64,2,16,128]{4,3,2,1,0:T(8,128)(2,1)}, bf16[2,64,2,16,128]{4,3,2,1,0:T(8,128)(2,1)S(1)}, u32[]{:S(2)}, u32[]{:S(2)}) collective-permute-start(bf16[2,64,2,16,128]{4,3,2,1,0:T(8,128)(2,1)} %get-tuple-element.23), channel_id=1, source_target_pairs={{0,1},{1,0},{2,3},{3,2},{4,5},{5,4},{6,7},{7,6},{8,9},{9,8},{10,11... | collective-permute-start | bytes 3145736 | tf_op jit(solution)/shard_map/ppermute | solution.py:296
  234.0 53.0 %collective-permute-start.4 = (bf16[2,64,2,16,128]{4,3,2,1,0:T(8,128)(2,1)}, bf16[2,64,2,16,128]{4,3,2,1,0:T(8,128)(2,1)S(1)}, u32[]{:S(2)}, u32[]{:S(2)}) collective-permute-start(bf16[2,64,2,16,128]{4,3,2,1,0:T(8,128)(2,1)} %get-tuple-element.24), channel_id=1, source_target_pairs={{0,1},{1,0},{2,3},{3,2},{4,5},{5,4},{6,7},{7,6},{8,9},{9,8},{10,11... | collective-permute-start | bytes 3145736 | tf_op jit(solution)/shard_map/ppermute | solution.py:296
  270.6 15.8 %copy-start.7 = (bf16[2,128,256]{2,1,0:T(8,128)(2,1)S(1)}, bf16[2,128,256]{2,1,0:T(8,128)(2,1)}, u32[]{:S(2)}) copy-start(bf16[2,128,256]{2,1,0:T(8,128)(2,1)} %constant.38) | copy-start | bytes 393220
  284.9 25.6 %collective-permute-start.1 = (bf16[2,64,2,16,128]{4,3,2,1,0:T(8,128)(2,1)}, bf16[2,64,2,16,128]{4,3,2,1,0:T(8,128)(2,1)}, u32[]{:S(2)}, u32[]{:S(2)}) collective-permute-start(bf16[2,64,2,16,128]{4,3,2,1,0:T(8,128)(2,1)} %get-tuple-element.21), channel_id=1, source_target_pairs={{0,1},{1,0},{2,3},{3,2},{4,5},{5,4},{6,7},{7,6},{8,9},{9,8},{10,11... | collective-permute-start | bytes 3145736 | tf_op jit(solution)/shard_map/ppermute | solution.py:296
  287.0 23.5 %copy-start.1 = (bf16[2,64,2,16,128]{4,3,2,1,0:T(8,128)(2,1)}, bf16[2,64,2,16,128]{4,3,2,1,0:T(8,128)(2,1)S(1)}, u32[]{:S(2)}) copy-start(bf16[2,64,2,16,128]{4,3,2,1,0:T(8,128)(2,1)S(1)} %collective-permute-done.2.refs_5_) | copy-start | bytes 3145732
  287.0 23.5 %copy-start.2 = (bf16[2,64,2,16,128]{4,3,2,1,0:T(8,128)(2,1)}, bf16[2,64,2,16,128]{4,3,2,1,0:T(8,128)(2,1)S(1)}, u32[]{:S(2)}) copy-start(bf16[2,64,2,16,128]{4,3,2,1,0:T(8,128)(2,1)S(1)} %collective-permute-done.3.refs_6_) | copy-start | bytes 3145732
  287.1 23.5 %copy-start.3 = (bf16[2,64,2,16,128]{4,3,2,1,0:T(8,128)(2,1)}, bf16[2,64,2,16,128]{4,3,2,1,0:T(8,128)(2,1)S(1)}, u32[]{:S(2)}) copy-start(bf16[2,64,2,16,128]{4,3,2,1,0:T(8,128)(2,1)S(1)} %collective-permute-done.4.refs_7_) | copy-start | bytes 3145732
Sparse Core Ops, SparseCore 0:
  65.1 52.1 all-gather.10
  119.4 48.8 all-gather.12
  170.5 49.0 all-gather.14
  221.6 48.8 all-gather.8

commit v2 on v1

--- a/solution.py
+++ b/solution.py
@@ -166,50 +166,198 @@
             )
 
 
-def score_kernel(rotations, groups, length, fx_ref, ix_ref, iy_ref, rec_ref, in_ref, mine_ref, other_ref, hold):
-    fx = fx_ref[...]
-    ix = ix_ref[...]
-    iy = iy_ref[...]
+def score_kernel(
+    rotations, groups, length, chunks, fx_ref, ix_ref, iy_ref, rec_ref, in_ref, mine_ref, far_ref,
+    held, rec, send, hold, rec_sem, own_sem, ring_out, ring_in, pair_out, pair_in, slab_out, slab_in,
+):
+    me = lax.axis_index("grp")
+    slab = lax.axis_index("slab")
+    core = lax.rem(me, 2)
+    height = groups // 4
+    around = groups // 2
+    row = me // 4
+    column = lax.rem(me // 2, 2)
+    spot = jnp.where(column == 0, row, around - 1 - row)
+
+    def device(at, which):
+        at = lax.rem(at + around, around)
+        return jnp.where(at < height, at * 4, (around - 1 - at) * 4 + 2) + which
+
+    beside = (device(spot + 1, core), device(spot - 1, core))
+    partner = device(spot, 1 - core)
+
+    def place(to):
+        return {"grp": to, "slab": slab}
+
+    across = {"grp": me, "slab": 1 - slab}
+    MESH = pl.DeviceIdType.MESH
+    load = pltpu.make_async_copy(rec_ref, rec, rec_sem)
+    load.start()
+    own = pltpu.make_async_copy(in_ref, held.at[me], own_sem)
+    own.start()
+    barrier = pltpu.get_barrier_semaphore()
+    for to in (place(beside[0]), place(beside[1]), place(partner), across):
+        pl.semaphore_signal(barrier, inc=1, device_id=to, device_id_type=MESH)
+    pl.semaphore_wait(barrier, 4)
+    own.wait()
+
+    def origin(d, t):
+        return spot - t if d == 0 else spot + t
+
+    def part(slot, c):
+        return held.at[slot, pl.ds(c * SUB, SUB)]
+
+    def ring(d, c, t, slot):
+        return pltpu.make_async_remote_copy(
+            src_ref=part(slot, c), dst_ref=part(slot, c),
+            send_sem=ring_out.at[d, c, t], recv_sem=ring_in.at[d, c, t],
+            device_id=place(beside[d]), device_id_type=MESH,
+        )
+
+    def ring_send(d, c, t):
+        ring(d, c, t, device(origin(d, t), core)).start()
+
+    def ring_wait(d, c, t):
+        ring(d, c, t, device(origin(d, t + 1), core)).wait_recv()
+
+    def pair(d, c, t, which):
+        slot = device(origin(d, t), which)
+        return pltpu.make_async_remote_copy(
+            src_ref=part(slot, c), dst_ref=part(slot, c),
+            send_sem=pair_out.at[d, c, t], recv_sem=pair_in.at[d, c, t],
+            device_id=place(partner), device_id_type=MESH,
+        )
+
+    def slab_copy(c):
+        return pltpu.make_async_remote_copy(
+            src_ref=send.at[c], dst_ref=far_ref.at[c],
+            send_sem=slab_out.at[c], recv_sem=slab_in.at[c],
+            device_id=across, device_id_type=MESH,
+        )
+
+    far_step = around // 2 - 1
+
+    def for_far(c, act):
+        for d in range(2):
+            @pl.when(lax.rem(c, 2) == d)
+            def _():
+                act(d)
+
+    def arrived(c, t):
+        for d in range(2):
+            ring_wait(d, c, t)
+            if t + 1 < far_step:
+                ring_send(d, c, t + 1)
+            pair(d, c, t + 1, core).start()
+
     rows = rotations * length
-
-    @pl.loop(0, SUB, unroll=2)
-    def _(k):
-        kr = [rec_ref[0, j, k].astype(f32) for j in range(2)]
-        ki = [rec_ref[1, j, k].astype(f32) for j in range(2)]
-        real, imag = [], []
-        for r in range(rotations):
-            cols = [
-                jnp.concatenate([in_ref[g, k, 2 * r + j] for g in range(groups)], 0) for j in range(2)
-            ]
-            spec = dot(fx, jnp.concatenate(cols, 1))
-            sr = [spec[:length, j * length : (j + 1) * length] for j in range(2)]
-            si = [spec[length:, j * length : (j + 1) * length] for j in range(2)]
-            real.append(kr[0] * sr[0] - ki[0] * si[0] + (kr[1] * sr[1] - ki[1] * si[1]))
-            imag.append(kr[0] * si[0] + ki[0] * sr[0] + (kr[1] * si[1] + ki[1] * sr[1]))
-        product = jnp.concatenate(
-            [jnp.concatenate(real, 1).astype(bf16), jnp.concatenate(imag, 1).astype(bf16)], 0
-        )
-        done = dot(ix, product).astype(bf16)
-        flat = []
-        for r in range(rotations):
-            at = slice(r * length, (r + 1) * length)
-            flat.append(jnp.concatenate([done[:length, at], done[length:, at]], 1))
-        planes = dot(jnp.concatenate(flat, 0), iy)
-        for p in range(2):
-            hold[p, pl.ds(k * rows, rows), :] = planes[:, p * length : (p + 1) * length]
-
     half = length // 2
 
-    @pl.loop(0, half, unroll=4)
-    def _(x):
-        for r in range(rotations):
-            for ref, first in ((mine_ref, 0), (other_ref, half)):
+    def compute(c, first):
+        @pl.loop(first, first + SUB // 2, unroll=2)
+        def _(k):
+            z = c * SUB + k
+            kr = [rec[0, j, z].astype(f32) for j in range(2)]
+            ki = [rec[1, j, z].astype(f32) for j in range(2)]
+            real, imag = [], []
+            for r in range(rotations):
+                cols = [
+                    jnp.concatenate([held[g, z, 2 * r + j] for g in range(groups)], 0)
+                    for j in range(2)
+                ]
+                spec = dot(fx_ref[...], jnp.concatenate(cols, 1))
+                sr = [spec[:length, j * length : (j + 1) * length] for j in range(2)]
+                si = [spec[length:, j * length : (j + 1) * length] for j in range(2)]
+                real.append(kr[0] * sr[0] - ki[0] * si[0] + (kr[1] * sr[1] - ki[1] * si[1]))
+                imag.append(kr[0] * si[0] + ki[0] * sr[0] + (kr[1] * si[1] + ki[1] * sr[1]))
+            product = jnp.concatenate(
+                [jnp.concatenate(real, 1).astype(bf16), jnp.concatenate(imag, 1).astype(bf16)], 0
+            )
+            done = dot(ix_ref[...], product).astype(bf16)
+            flat = []
+            for r in range(rotations):
+                at = slice(r * length, (r + 1) * length)
+                flat.append(jnp.concatenate([done[:length, at], done[length:, at]], 1))
+            planes = dot(jnp.concatenate(flat, 0), iy_ref[...])
+            for p in range(2):
+                hold[p, pl.ds(k * rows, rows), :] = planes[:, p * length : (p + 1) * length]
+
+    def collect(c, ref, first):
+        @pl.loop(0, half, unroll=4)
+        def _(x):
+            for r in range(rotations):
                 at = pl.ds(r * length + first + x, SUB, stride=rows)
-                ref[r, x, 0] = jnp.concatenate([hold[0, at, :], hold[1, at, :]], 0).astype(bf16)
-
-
-def last_kernel(rotations, count, length, wide, mz_ref, *refs):
-    ins, out_ref, hold = refs[: 2 * count], refs[-2], refs[-1]
+                ref[c, r, x] = jnp.concatenate([hold[0, at, :], hold[1, at, :]], 0).astype(bf16)
+
+    @pl.loop(0, chunks + 3)
+    def _(i):
+        c1, c2, c3 = i - 1, i - 2, i - 3
+
+        @pl.when(i < chunks)
+        def _():
+            for d in range(2):
+                ring_send(d, i, 0)
+            pair(0, i, 0, core).start()
+
+        @pl.when((c1 >= 0) & (c1 < chunks))
+        def _():
+            arrived(c1, 1)
+
+        @pl.when((c2 >= 0) & (c2 < chunks))
+        def _():
+            def act(d):
+                ring_wait(d, c2, far_step)
+                pair(d, c2, far_step + 1, core).start()
+
+            for_far(c2, act)
+
+        @pl.when(i == 2)
+        def _():
+            load.wait()
+
+        @pl.when(c3 >= 0)
+        def _():
+            compute(c3, SUB // 2)
+            collect(c3, send, half)
+            collect(c3, mine_ref, 0)
+            slab_copy(c3).start()
+
+        @pl.when(i < chunks)
+        def _():
+            arrived(i, 0)
+
+        @pl.when((c1 >= 0) & (c1 < chunks))
+        def _():
+            arrived(c1, 2)
+            for_far(c1, lambda d: ring_send(d, c1, far_step))
+
+        @pl.when((c2 >= 0) & (c2 < chunks))
+        def _():
+            pair(0, c2, 0, 1 - core).wait_recv()
+            for t in range(1, far_step + 1):
+                for d in range(2):
+                    pair(d, c2, t, 1 - core).wait_recv()
+            for_far(c2, lambda d: pair(d, c2, far_step + 1, 1 - core).wait_recv())
+            compute(c2, 0)
+
+    @pl.loop(0, chunks)
+    def _(c):
+        for t in range(far_step):
+            for d in range(2):
+                ring(d, c, t, device(origin(d, t), core)).wait_send()
+                pair(d, c, t + 1, core).wait_send()
+        pair(0, c, 0, core).wait_send()
+
+        def act(d):
+            ring(d, c, far_step, device(origin(d, far_step), core)).wait_send()
+            pair(d, c, far_step + 1, core).wait_send()
+
+        for_far(c, act)
+        slab_copy(c).wait_send()
+        slab_copy(c).wait_recv()
+
+
+def last_kernel(rotations, length, wide, mz_ref, mine_ref, far_ref, out_ref, hold):
     mz = mz_ref[...]
 
     @pl.loop(0, wide, unroll=2)
@@ -217,8 +365,8 @@
         cols = []
         for r in range(rotations):
             tiles = []
-            for ref in ins:
-                tiles += [ref[r, x, t] for t in range(ref.shape[2])]
+            for ref in (mine_ref, far_ref):
+                tiles += [ref[t, r, x] for t in range(ref.shape[0])]
             cols.append(jnp.concatenate(tiles, 0))
         scores = dot(mz, jnp.concatenate(cols, 1))
         best = scores[:, :length]
@@ -229,9 +377,6 @@
     @pl.loop(0, length, unroll=4)
     def _(z):
         out_ref[z] = hold[pl.ds(z, wide, stride=length), :].astype(bf16)
-
-
-CHUNKS = 4
 
 
 def quick_body(groups, ligand_grids, receptor_kernel):
@@ -269,42 +414,44 @@
     joined = jnp.concatenate([mine, came], axis=2)
 
     rec = receptor_kernel[0]
-    chunk = half // CHUNKS
-    steps = chunk // SUB
-    own_parts, far_parts = [], []
-    for c in range(CHUNKS):
-        gathered = lax.all_gather(joined[c * chunk : (c + 1) * chunk], "grp", axis=0, tiled=False)
-        part = jax.ShapeDtypeStruct((rotations, half, steps, TILE, length), bf16)
-        keep, send = pl.pallas_call(
-            functools.partial(score_kernel, rotations, groups, length),
-            grid=(steps,),
-            out_shape=[part, part],
-            in_specs=[
-                pl.BlockSpec((side, side), lambda t: (0, 0)),
-                pl.BlockSpec((side, side), lambda t: (0, 0)),
-                pl.BlockSpec((side, side), lambda t: (0, 0)),
-                pl.BlockSpec((2, pairs, SUB, length, length), lambda t, c=c: (0, 0, c * steps + t, 0, 0)),
-                pl.BlockSpec((groups, SUB, grids, TILE, length), lambda t: (0, t, 0, 0, 0)),
-            ],
-            out_specs=[pl.BlockSpec((rotations, half, 1, TILE, length), lambda t: (0, 0, t, 0, 0))] * 2,
-            scratch_shapes=[pltpu.VMEM((2, SUB * rotations * length, length), f32)],
-            cost_estimate=pl.CostEstimate(
-                flops=chunk * 4 * 2 * side**3, bytes_accessed=10 * 2**20, transcendentals=0
-            ),
-        )(fx, ix, iy, rec, gathered)
-        own_parts.append(keep)
-        far_parts.append(lax.ppermute(send, "slab", swap))
+    chunks = half // SUB
+    hops = groups // 4
+    part = jax.ShapeDtypeStruct((chunks, rotations, half, TILE, length), bf16)
+    dma = pltpu.SemaphoreType.DMA
+    keep, far = pl.pallas_call(
+        functools.partial(score_kernel, rotations, groups, length, chunks),
+        out_shape=[part, part],
+        in_specs=[whole] * 3 + [pl.BlockSpec(memory_space=pl.ANY), whole],
+        out_specs=[whole] * 2,
+        scratch_shapes=[
+            pltpu.VMEM((groups,) + joined.shape, bf16),
+            pltpu.VMEM(rec.shape, bf16),
+            pltpu.VMEM(part.shape, bf16),
+            pltpu.VMEM((2, SUB * rotations * length, length), f32),
+            dma,
+            dma,
+            dma((2, chunks, hops)),
+            dma((2, chunks, hops)),
+            dma((2, chunks, hops + 1)),
+            dma((2, chunks, hops + 1)),
+            dma((chunks,)),
+            dma((chunks,)),
+        ],
+        compiler_params=pltpu.CompilerParams(
+            collective_id=0, has_side_effects=True, vmem_limit_bytes=60 * 2**20
+        ),
+    )(fx, ix, iy, rec, joined)
 
     wide = TILE
     best = pl.pallas_call(
-        functools.partial(last_kernel, rotations, CHUNKS, length, wide),
+        functools.partial(last_kernel, rotations, length, wide),
         grid=(half // wide,),
         out_shape=jax.ShapeDtypeStruct((length, half, length), bf16),
         in_specs=[pl.BlockSpec((length, side), lambda t: (0, 0))]
-        + [pl.BlockSpec((rotations, wide, steps, TILE, length), lambda t: (0, t, 0, 0, 0))] * (2 * CHUNKS),
+        + [pl.BlockSpec((chunks, rotations, wide, TILE, length), lambda t: (0, 0, t, 0, 0))] * 2,
         out_specs=pl.BlockSpec((length, wide, length), lambda t: (0, t, 0)),
         scratch_shapes=[pltpu.VMEM((wide * length, length), f32)],
-    )(mz, *own_parts, *far_parts)
+    )(mz, keep, far)
     return best[None]
 
 
@@ -318,7 +465,8 @@
         and width % groups == 0
         and 4 * (width // groups) == TILE
         and length % 128 == 0
-        and (length // 2) % (CHUNKS * SUB) == 0
+        and (length // 2) % SUB == 0
+        and groups == 4 * 4
     )
     if fits:
         return quick_body(groups, ligand_grids, receptor_kernel)

time: 329 us -> 206 us (0.63)
  waiting for transfers between devices: 215 us -> 34 us
  Pallas kernels: 80.5 us -> 158 us
  between operations: 13.2 us -> 0.04 us
  starting transfers between devices: 15.1 us -> 9.04 us
    all_gather x4 -> x0, waiting for transfers between devices: 155 us -> none  [quick_body(): lax.all_gather(joined[c * chunk:(c + 1) * chunk], 'grp', axis=0, tiled=Fa...]
    pallas_call x5 -> x2, Pallas kernels: 69.4 us -> 147 us  [the longest x1 135 us: quick_body(): pl.pallas_call(functools.partial(score_kernel, rotations, groups, length,...]
    ppermute x4 -> x0, waiting for transfers between devices: 23.5 us -> none  [quick_body(): far_parts.append(lax.ppermute(send, 'slab', swap))]
    ppermute x4 -> x0, starting transfers between devices: 5.9 us -> none  [quick_body(): far_parts.append(lax.ppermute(send, 'slab', swap))]
  transfers between devices with their start and end apart: 10 -> 2, of which waited for: 7 -> 2; matrix products, arithmetic and copies ran while one was open for 1% -> 1% of each run, Pallas kernels for 17% -> 0%
where the time goes in v2:
time: 206 us
  Pallas kernels  158 us (77%)
  waiting for transfers between devices  34 us (17%)
  starting transfers between devices  9.04 us (4%)
  local copies, waits for them, and re-layouts  3.05 us (1%)
  other arithmetic  2.19 us (1%)
    pallas_call x1, Pallas kernels, quick_body(): pl.pallas_call(functools.partial(score_kernel, rotations, groups, length,...  135 us
    all_to_all x1, waiting for transfers between devices, quick_body(): lax.all_to_all(blocks, 'grp', split_axis=0, concat_axis=0, tiled=True)  22.2 us
    ppermute x1, waiting for transfers between devices, quick_body(): came = lax.ppermute(other, 'slab', swap)  11.8 us
    pallas_call x1, Pallas kernels, quick_body(): pl.pallas_call(functools.partial(last_kernel, rotations, length, wide), g...  11.8 us
    all_to_all x1, starting transfers between devices, quick_body(): lax.all_to_all(blocks, 'grp', split_axis=0, concat_axis=0, tiled=True)  7.52 us
    pallas_call x1, Pallas kernels, quick_body(): pl.pallas_call(functools.partial(zy_kernel, rotations, groups, block, len...  6.02 us
    pallas_call x1, Pallas kernels, quick_body(): pl.pallas_call(functools.partial(split_kernel, rotations, pairs, depth, w...  5.06 us
  transfers between devices with their start and end apart: 2, of which 2 were waited for; matrix products, arithmetic and copies ran while one was open for 1% of the time, Pallas kernels for 0%

profile of v2, /device:TPU:0, one launch (start us, length us, event | category | flops | bytes accessed | tf_op | source)
XLA Modules:
  0.0 206.0 jit_solution(2225256743925778501)
XLA Ops:
  0.0 0.0 copy-start.3
  0.0 5.1 %shard_map.82 = bf16[16,4,4,16,128]{4,3,2,1,0:T(8,128)(2,1)} custom-call(f32[4096,128]{1,0:T(8,128)} %bitcast.12), custom_call_target="tpu_custom_call" | custom-call | tf_op jit(solution)/shard_map/pallas_call | solution.py:397
  5.1 0.0 copy-start.4
  5.1 0.0 copy-start.1
  5.1 0.0 copy-start.2
  5.1 7.5 %all-to-all-start = ((bf16[16,4,4,16,128]{4,3,2,1,0:T(8,128)(2,1)}), bf16[16,4,4,16,128]{4,3,2,1,0:T(8,128)(2,1)S(1)}, u32[]{:S(2)}, u32[]{:S(2)}) async-start(bf16[16,4,4,16,128]{4,3,2,1,0:T(8,128)(2,1)} %shard_map.82), calls=%async_computation | async-start | bytes 2097152 | tf_op jit(solution)/shard_map/all_to_all | solution.py:403
  12.6 0.0 copy-done.3
  12.6 0.7 dynamic-slice_bitcast_fusion.fz_ref
  13.3 22.2 %all-to-all-done.in_ref = bf16[16,4,4,16,128]{4,3,2,1,0:T(8,128)(2,1)S(1)} async-done(((bf16[16,4,4,16,128]{4,3,2,1,0:T(8,128)(2,1)}), bf16[16,4,4,16,128]{4,3,2,1,0:T(8,128)(2,1)S(1)}, u32[]{:S(2)}, u32[]{:S(2)}) %all-to-all-start) | async-done | bytes 1048608 | tf_op jit(solution)/shard_map/all_to_all | solution.py:403
  35.5 0.0 copy-start
  35.5 1.0 copy-done
  36.5 6.0 %shard_map.83 = (bf16[64,4,8,128]{3,2,1,0:T(8,128)(2,1)}, bf16[64,4,8,128]{3,2,1,0:T(8,128)(2,1)}) custom-call(bf16[256,256]{1,0:T(8,128)(2,1)} %dynamic-slice_bitcast_fusion.fz_ref, bf16[256,256]{1,0:T(8,128)(2,1)} %constant.43.fy_ref, bf16[16,4,4,16,128]{4,3,2,1,0:T(8,128)(2,1)} %copy-done), custom_call_target="tpu_custom_call" | custom-call | tf_op jit(solution)/shard_map/pallas_call | solution.py:405
  42.5 1.5 collective-permute-start
  44.0 0.0 copy-done.4
  44.0 0.6 dynamic-slice_bitcast_fusion.3.mz_ref
  44.6 0.0 copy-done.1
  44.6 0.0 copy-done.2
  44.6 0.8 dynamic-slice_bitcast_fusion.1
  45.4 11.8 %collective-permute-done = bf16[64,4,8,128]{3,2,1,0:T(8,128)(2,1)S(1)} collective-permute-done((bf16[64,4,8,128]{3,2,1,0:T(8,128)(2,1)}, bf16[64,4,8,128]{3,2,1,0:T(8,128)(2,1)S(1)}, u32[]{:S(2)}, u32[]{:S(2)}) %collective-permute-start) | collective-permute-done | bytes 524320 | tf_op jit(solution)/shard_map/ppermute | solution.py:413
  57.2 2.2 %pad_maximum_fusion.in_ref = bf16[64,4,16,128]{3,2,1,0:T(8,128)(2,1)} fusion(bf16[64,4,8,128]{3,2,1,0:T(8,128)(2,1)S(1)} %collective-permute-done, bf16[64,4,8,128]{3,2,1,0:T(8,128)(2,1)} %get-tuple-element.9), kind=kLoop, calls=%fused_computation | loop fusion | flops 2097152 | bytes 2097152 | tf_op jit(solution)/shard_map/concatenate | solution.py:414
  59.4 134.7 %shard_map.84 = (bf16[8,2,64,16,128]{4,3,2,1,0:T(8,128)(2,1)}, bf16[8,2,64,16,128]{4,3,2,1,0:T(8,128)(2,1)}) custom-call(bf16[256,256]{1,0:T(8,128)(2,1)} %get-tuple-element.14.fx_ref, bf16[256,256]{1,0:T(8,128)(2,1)} %get-tuple-element.13.ix_ref, bf16[256,256]{1,0:T(8,128)(2,1)} %constant.41.iy_ref, bf16[2,2,64,128,128]{4,3,2,1,0:T(8,128)(2,1)} %bitcast.11, ...), custom_call_target="tpu_custom_call" | custom-call | tf_op jit(solution)/shard_map/pallas_call | solution.py:421
  194.2 11.8 %shard_map.85 = bf16[128,64,128]{2,1,0:T(8,128)(2,1)} custom-call(bf16[128,256]{1,0:T(8,128)(2,1)} %dynamic-slice_bitcast_fusion.3.mz_ref, bf16[8,2,64,16,128]{4,3,2,1,0:T(8,128)(2,1)} %get-tuple-element.11.mine_ref, bf16[8,2,64,16,128]{4,3,2,1,0:T(8,128)(2,1)} %get-tuple-element.12.far_ref), custom_call_target="tpu_custom_call" | custom-call | tf_op jit(solution)/shard_map/pallas_call | solution.py:446
Async XLA Ops:
  0.0 12.6 %copy-start.3 = (bf16[2,256,256]{2,1,0:T(8,128)(2,1)S(1)}, bf16[2,256,256]{2,1,0:T(8,128)(2,1)}, u32[]{:S(2)}) copy-start(bf16[2,256,256]{2,1,0:T(8,128)(2,1)} %constant.42) | copy-start | bytes 786436
  5.1 38.9 %copy-start.4 = (bf16[2,128,256]{2,1,0:T(8,128)(2,1)S(1)}, bf16[2,128,256]{2,1,0:T(8,128)(2,1)}, u32[]{:S(2)}) copy-start(bf16[2,128,256]{2,1,0:T(8,128)(2,1)} %constant.38) | copy-start | bytes 393220
  5.1 39.6 %copy-start.1 = (bf16[2,256,256]{2,1,0:T(8,128)(2,1)S(1)}, bf16[2,256,256]{2,1,0:T(8,128)(2,1)}, u32[]{:S(2)}) copy-start(bf16[2,256,256]{2,1,0:T(8,128)(2,1)} %constant.40) | copy-start | bytes 786436
  5.1 39.6 %copy-start.2 = (bf16[2,256,256]{2,1,0:T(8,128)(2,1)S(1)}, bf16[2,256,256]{2,1,0:T(8,128)(2,1)}, u32[]{:S(2)}) copy-start(bf16[2,256,256]{2,1,0:T(8,128)(2,1)} %constant.39) | copy-start | bytes 786436
  5.1 30.4 %all-to-all-start = ((bf16[16,4,4,16,128]{4,3,2,1,0:T(8,128)(2,1)}), bf16[16,4,4,16,128]{4,3,2,1,0:T(8,128)(2,1)S(1)}, u32[]{:S(2)}, u32[]{:S(2)}) async-start(bf16[16,4,4,16,128]{4,3,2,1,0:T(8,128)(2,1)} %shard_map.82), calls=%async_computation | async-start | bytes 2097152 | tf_op jit(solution)/shard_map/all_to_all | solution.py:403
  35.5 1.0 copy-start
  42.5 14.7 %collective-permute-start = (bf16[64,4,8,128]{3,2,1,0:T(8,128)(2,1)}, bf16[64,4,8,128]{3,2,1,0:T(8,128)(2,1)S(1)}, u32[]{:S(2)}, u32[]{:S(2)}) collective-permute-start(bf16[64,4,8,128]{3,2,1,0:T(8,128)(2,1)} %get-tuple-element.10), channel_id=1, source_target_pairs={{0,1},{1,0},{2,3},{3,2},{4,5},{5,4},{6,7},{7,6},{8,9},{9,8},{10,11... | collective-permute-start | bytes 1572872 | tf_op jit(solution)/shard_map/ppermute | solution.py:413

commit v3 on v2

--- a/solution.py
+++ b/solution.py
@@ -167,8 +167,8 @@
 
 
 def score_kernel(
-    rotations, groups, length, chunks, fx_ref, ix_ref, iy_ref, rec_ref, in_ref, mine_ref, far_ref,
-    held, rec, send, hold, rec_sem, own_sem, ring_out, ring_in, pair_out, pair_in, slab_out, slab_in,
+    rotations, groups, length, chunks, fx_ref, ix_ref, iy_ref, rec_ref, near_ref, swap_ref, mine_ref, far_ref,
+    held, came, rec, send, hold, rec_sem, swap_out, swap_in, ring_out, ring_in, pair_out, pair_in, slab_out, slab_in,
 ):
     me = lax.axis_index("grp")
     slab = lax.axis_index("slab")
@@ -193,13 +193,34 @@
     MESH = pl.DeviceIdType.MESH
     load = pltpu.make_async_copy(rec_ref, rec, rec_sem)
     load.start()
-    own = pltpu.make_async_copy(in_ref, held.at[me], own_sem)
-    own.start()
     barrier = pltpu.get_barrier_semaphore()
     for to in (place(beside[0]), place(beside[1]), place(partner), across):
         pl.semaphore_signal(barrier, inc=1, device_id=to, device_id_type=MESH)
     pl.semaphore_wait(barrier, 4)
-    own.wait()
+
+    def swap(c):
+        at = pl.ds(c * SUB, SUB)
+        return pltpu.make_async_remote_copy(
+            src_ref=swap_ref.at[at], dst_ref=came.at[at],
+            send_sem=swap_out.at[c], recv_sem=swap_in.at[c],
+            device_id=across, device_id_type=MESH,
+        )
+
+    @pl.loop(0, chunks)
+    def _(c):
+        swap(c).start()
+
+    def join(c):
+        swap(c).wait_recv()
+
+        @pl.loop(0, SUB)
+        def _(k):
+            z = c * SUB + k
+            for g in range(near_ref.shape[1]):
+                both = [near_ref[z, g].astype(f32), came[z, g].astype(f32)]
+                held[me, z, g] = jnp.concatenate(both, 0).astype(bf16)
+
+    join(0)
 
     def origin(d, t):
         return spot - t if d == 0 else spot + t
@@ -289,56 +310,64 @@
                 at = pl.ds(r * length + first + x, SUB, stride=rows)
                 ref[c, r, x] = jnp.concatenate([hold[0, at, :], hold[1, at, :]], 0).astype(bf16)
 
-    @pl.loop(0, chunks + 3)
+    @pl.loop(0, chunks + 2)
     def _(i):
-        c1, c2, c3 = i - 1, i - 2, i - 3
-
-        @pl.when(i < chunks)
-        def _():
+        c1, c2 = i - 1, i - 2
+
+        def open_chunk():
             for d in range(2):
                 ring_send(d, i, 0)
             pair(0, i, 0, core).start()
 
+        @pl.when((i < chunks) & (i != 1))
+        def _():
+            open_chunk()
+
         @pl.when((c1 >= 0) & (c1 < chunks))
         def _():
             arrived(c1, 1)
 
-        @pl.when((c2 >= 0) & (c2 < chunks))
+        @pl.when(i == 1)
+        def _():
+            open_chunk()
+
+        @pl.when(i == 2)
+        def _():
+            load.wait()
+
+        @pl.when(c2 >= 0)
         def _():
             def act(d):
                 ring_wait(d, c2, far_step)
                 pair(d, c2, far_step + 1, core).start()
 
             for_far(c2, act)
-
-        @pl.when(i == 2)
-        def _():
-            load.wait()
-
-        @pl.when(c3 >= 0)
-        def _():
-            compute(c3, SUB // 2)
-            collect(c3, send, half)
-            collect(c3, mine_ref, 0)
-            slab_copy(c3).start()
-
-        @pl.when(i < chunks)
-        def _():
-            arrived(i, 0)
-
-        @pl.when((c1 >= 0) & (c1 < chunks))
-        def _():
-            arrived(c1, 2)
-            for_far(c1, lambda d: ring_send(d, c1, far_step))
-
-        @pl.when((c2 >= 0) & (c2 < chunks))
-        def _():
             pair(0, c2, 0, 1 - core).wait_recv()
             for t in range(1, far_step + 1):
                 for d in range(2):
                     pair(d, c2, t, 1 - core).wait_recv()
             for_far(c2, lambda d: pair(d, c2, far_step + 1, 1 - core).wait_recv())
             compute(c2, 0)
+
+        @pl.when(i < chunks)
+        def _():
+            arrived(i, 0)
+
+        @pl.when((c1 >= 0) & (c1 < chunks))
+        def _():
+            arrived(c1, 2)
+            for_far(c1, lambda d: ring_send(d, c1, far_step))
+
+        @pl.when(i + 1 < chunks)
+        def _():
+            join(i + 1)
+
+        @pl.when(c2 >= 0)
+        def _():
+            compute(c2, SUB // 2)
+            collect(c2, send, half)
+            collect(c2, mine_ref, 0)
+            slab_copy(c2).start()
 
     @pl.loop(0, chunks)
     def _(c):
@@ -353,6 +382,7 @@
             pair(d, c, far_step + 1, core).wait_send()
 
         for_far(c, act)
+        swap(c).wait_send()
         slab_copy(c).wait_send()
         slab_copy(c).wait_recv()
 
@@ -409,9 +439,6 @@
         out_specs=[whole] * 2,
         scratch_shapes=[pltpu.VMEM((2 * block * grids * length, length), f32)],
     )(fz, fy, lines)
-    swap = [(0, 1), (1, 0)]
-    came = lax.ppermute(other, "slab", swap)
-    joined = jnp.concatenate([mine, came], axis=2)
 
     rec = receptor_kernel[0]
     chunks = half // SUB
@@ -421,15 +448,17 @@
     keep, far = pl.pallas_call(
         functools.partial(score_kernel, rotations, groups, length, chunks),
         out_shape=[part, part],
-        in_specs=[whole] * 3 + [pl.BlockSpec(memory_space=pl.ANY), whole],
+        in_specs=[whole] * 3 + [pl.BlockSpec(memory_space=pl.ANY), whole, whole],
         out_specs=[whole] * 2,
         scratch_shapes=[
-            pltpu.VMEM((groups,) + joined.shape, bf16),
+            pltpu.VMEM((groups, half, grids, TILE, length), bf16),
+            pltpu.VMEM(other.shape, bf16),
             pltpu.VMEM(rec.shape, bf16),
             pltpu.VMEM(part.shape, bf16),
             pltpu.VMEM((2, SUB * rotations * length, length), f32),
             dma,
-            dma,
+            dma((chunks,)),
+            dma((chunks,)),
             dma((2, chunks, hops)),
             dma((2, chunks, hops)),
             dma((2, chunks, hops + 1)),
@@ -440,7 +469,7 @@
         compiler_params=pltpu.CompilerParams(
             collective_id=0, has_side_effects=True, vmem_limit_bytes=60 * 2**20
         ),
-    )(fx, ix, iy, rec, joined)
+    )(fx, ix, iy, rec, mine, other)
 
     wide = TILE
     best = pl.pallas_call(

time: 206 us -> 194 us (0.942)
  waiting for transfers between devices: 34 us -> 20.8 us
  Pallas kernels: 158 us -> 163 us
  other arithmetic: 2.19 us -> 0 us
    ppermute x1 -> x0, waiting for transfers between devices: 11.8 us -> none  [quick_body(): came = lax.ppermute(other, 'slab', swap)]
    pallas_call x1, Pallas kernels: 135 us -> 140 us  [quick_body(): pl.pallas_call(functools.partial(score_kernel, rotations, groups, length,...]
    concatenate x1 -> x0, other arithmetic: 2.19 us -> none  [quick_body(): joined = jnp.concatenate([mine, came], axis=2)]
  transfers between devices with their start and end apart: 2 -> 1, of which waited for: 2 -> 1; matrix products, arithmetic and copies ran while one was open for 1% -> 1% of each run, Pallas kernels for 0% -> 0%
where the time goes in v3:
time: 194 us
  Pallas kernels  163 us (84%)
  waiting for transfers between devices  20.8 us (11%)
  starting transfers between devices  7.4 us (4%)
  local copies, waits for them, and re-layouts  3.01 us (2%)
    pallas_call x1, Pallas kernels, quick_body(): pl.pallas_call(functools.partial(score_kernel, rotations, groups, length,...  140 us
    all_to_all x1, waiting for transfers between devices, quick_body(): lax.all_to_all(blocks, 'grp', split_axis=0, concat_axis=0, tiled=True)  20.8 us
    pallas_call x1, Pallas kernels, quick_body(): pl.pallas_call(functools.partial(last_kernel, rotations, length, wide), g...  11.8 us
    all_to_all x1, starting transfers between devices, quick_body(): lax.all_to_all(blocks, 'grp', split_axis=0, concat_axis=0, tiled=True)  7.4 us
    pallas_call x1, Pallas kernels, quick_body(): pl.pallas_call(functools.partial(zy_kernel, rotations, groups, block, len...  6.1 us
    pallas_call x1, Pallas kernels, quick_body(): pl.pallas_call(functools.partial(split_kernel, rotations, pairs, depth, w...  5.09 us
  transfers between devices with their start and end apart: 1, of which 1 were waited for; matrix products, arithmetic and copies ran while one was open for 1% of the time, Pallas kernels for 0%

profile of v3, /device:TPU:0, one launch (start us, length us, event | category | flops | bytes accessed | tf_op | source)
XLA Modules:
  0.0 194.0 jit_solution(12338925522714347590)
XLA Ops:
  0.0 0.0 copy-start.4
  0.0 0.0 copy-start.3
  0.0 0.0 copy-start.1
  0.0 0.0 copy-start.2
  0.0 5.1 %shard_map.82 = bf16[16,4,4,16,128]{4,3,2,1,0:T(8,128)(2,1)} custom-call(f32[4096,128]{1,0:T(8,128)} %bitcast.12), custom_call_target="tpu_custom_call" | custom-call | tf_op jit(solution)/shard_map/pallas_call | solution.py:427
  5.1 7.4 %all-to-all-start = ((bf16[16,4,4,16,128]{4,3,2,1,0:T(8,128)(2,1)}), bf16[16,4,4,16,128]{4,3,2,1,0:T(8,128)(2,1)S(1)}, u32[]{:S(2)}, u32[]{:S(2)}) async-start(bf16[16,4,4,16,128]{4,3,2,1,0:T(8,128)(2,1)} %shard_map.82), calls=%async_computation | async-start | bytes 2097152 | tf_op jit(solution)/shard_map/all_to_all | solution.py:433
  12.5 0.0 copy-done.4
  12.5 0.6 dynamic-slice_bitcast_fusion.3.mz_ref
  13.2 0.0 copy-done.3
  13.2 0.7 dynamic-slice_bitcast_fusion.2.fx_ref
  13.8 0.0 copy-done.1
  13.8 0.0 copy-done.2
  13.8 0.7 dynamic-slice_bitcast_fusion
  14.6 20.8 %all-to-all-done.in_ref = bf16[16,4,4,16,128]{4,3,2,1,0:T(8,128)(2,1)S(1)} async-done(((bf16[16,4,4,16,128]{4,3,2,1,0:T(8,128)(2,1)}), bf16[16,4,4,16,128]{4,3,2,1,0:T(8,128)(2,1)S(1)}, u32[]{:S(2)}, u32[]{:S(2)}) %all-to-all-start) | async-done | bytes 1048608 | tf_op jit(solution)/shard_map/all_to_all | solution.py:433
  35.4 0.0 copy-start
  35.4 1.0 copy-done
  36.4 6.1 %shard_map.83 = (bf16[64,4,8,128]{3,2,1,0:T(8,128)(2,1)}, bf16[64,4,8,128]{3,2,1,0:T(8,128)(2,1)}) custom-call(bf16[256,256]{1,0:T(8,128)(2,1)} %get-tuple-element.13.fz_ref, bf16[256,256]{1,0:T(8,128)(2,1)} %constant.43.fy_ref, bf16[16,4,4,16,128]{4,3,2,1,0:T(8,128)(2,1)} %copy-done), custom_call_target="tpu_custom_call" | custom-call | tf_op jit(solution)/shard_map/pallas_call | solution.py:435
  42.5 139.7 %shard_map.84 = (bf16[8,2,64,16,128]{4,3,2,1,0:T(8,128)(2,1)}, bf16[8,2,64,16,128]{4,3,2,1,0:T(8,128)(2,1)}) custom-call(bf16[256,256]{1,0:T(8,128)(2,1)} %dynamic-slice_bitcast_fusion.2.fx_ref, bf16[256,256]{1,0:T(8,128)(2,1)} %get-tuple-element.14.ix_ref, bf16[256,256]{1,0:T(8,128)(2,1)} %constant.41.iy_ref, bf16[2,2,64,128,128]{4,3,2,1,0:T(8,128)(2,1)} %bitcast.11, ...), custom_call_target="tpu_custom_call" | custom-call | tf_op jit(solution)/shard_map/pallas_call | solution.py:448
  182.2 11.8 %shard_map.85 = bf16[128,64,128]{2,1,0:T(8,128)(2,1)} custom-call(bf16[128,256]{1,0:T(8,128)(2,1)} %dynamic-slice_bitcast_fusion.3.mz_ref, bf16[8,2,64,16,128]{4,3,2,1,0:T(8,128)(2,1)} %get-tuple-element.11.mine_ref, bf16[8,2,64,16,128]{4,3,2,1,0:T(8,128)(2,1)} %get-tuple-element.12.far_ref), custom_call_target="tpu_custom_call" | custom-call | tf_op jit(solution)/shard_map/pallas_call | solution.py:475
Async XLA Ops:
  0.0 12.5 %copy-start.4 = (bf16[2,128,256]{2,1,0:T(8,128)(2,1)S(1)}, bf16[2,128,256]{2,1,0:T(8,128)(2,1)}, u32[]{:S(2)}) copy-start(bf16[2,128,256]{2,1,0:T(8,128)(2,1)} %constant.38) | copy-start | bytes 393220
  0.0 13.2 %copy-start.3 = (bf16[2,256,256]{2,1,0:T(8,128)(2,1)S(1)}, bf16[2,256,256]{2,1,0:T(8,128)(2,1)}, u32[]{:S(2)}) copy-start(bf16[2,256,256]{2,1,0:T(8,128)(2,1)} %constant.39) | copy-start | bytes 786436
  0.0 13.8 %copy-start.1 = (bf16[2,256,256]{2,1,0:T(8,128)(2,1)S(1)}, bf16[2,256,256]{2,1,0:T(8,128)(2,1)}, u32[]{:S(2)}) copy-start(bf16[2,256,256]{2,1,0:T(8,128)(2,1)} %constant.42) | copy-start | bytes 786436
  0.0 13.8 %copy-start.2 = (bf16[2,256,256]{2,1,0:T(8,128)(2,1)S(1)}, bf16[2,256,256]{2,1,0:T(8,128)(2,1)}, u32[]{:S(2)}) copy-start(bf16[2,256,256]{2,1,0:T(8,128)(2,1)} %constant.40) | copy-start | bytes 786436
  5.1 30.3 %all-to-all-start = ((bf16[16,4,4,16,128]{4,3,2,1,0:T(8,128)(2,1)}), bf16[16,4,4,16,128]{4,3,2,1,0:T(8,128)(2,1)S(1)}, u32[]{:S(2)}, u32[]{:S(2)}) async-start(bf16[16,4,4,16,128]{4,3,2,1,0:T(8,128)(2,1)} %shard_map.82), calls=%async_computation | async-start | bytes 2097152 | tf_op jit(solution)/shard_map/all_to_all | solution.py:433
  35.4 1.0 copy-start

commit v4 on v3

--- a/solution.py
+++ b/solution.py
@@ -167,8 +167,8 @@
 
 
 def score_kernel(
-    rotations, groups, length, chunks, fx_ref, ix_ref, iy_ref, rec_ref, near_ref, swap_ref, mine_ref, far_ref,
-    held, came, rec, send, hold, rec_sem, swap_out, swap_in, ring_out, ring_in, pair_out, pair_in, slab_out, slab_in,
+    rotations, groups, length, chunks, fx_ref, ix_ref, iy_ref, mz_ref, rec_ref, near_ref, swap_ref, out_ref,
+    mine_ref, far_ref, held, came, rec, send, hold, rec_sem, swap_out, swap_in, ring_out, ring_in, pair_out, pair_in, slab_out, slab_in,
 ):
     me = lax.axis_index("grp")
     slab = lax.axis_index("slab")
@@ -220,8 +220,6 @@
                 both = [near_ref[z, g].astype(f32), came[z, g].astype(f32)]
                 held[me, z, g] = jnp.concatenate(both, 0).astype(bf16)
 
-    join(0)
-
     def origin(d, t):
         return spot - t if d == 0 else spot + t
 
@@ -249,10 +247,11 @@
             device_id=place(partner), device_id_type=MESH,
         )
 
-    def slab_copy(c):
+    def slab_copy(c, q):
+        at = pl.ds(pl.multiple_of(q * TILE, TILE), TILE)
         return pltpu.make_async_remote_copy(
-            src_ref=send.at[c], dst_ref=far_ref.at[c],
-            send_sem=slab_out.at[c], recv_sem=slab_in.at[c],
+            src_ref=send.at[c, :, at], dst_ref=far_ref.at[c, :, at],
+            send_sem=slab_out.at[c, q], recv_sem=slab_in.at[c, q],
             device_id=across, device_id_type=MESH,
         )
 
@@ -310,26 +309,25 @@
                 at = pl.ds(r * length + first + x, SUB, stride=rows)
                 ref[c, r, x] = jnp.concatenate([hold[0, at, :], hold[1, at, :]], 0).astype(bf16)
 
+    def open_chunk(c):
+        for d in range(2):
+            ring_send(d, c, 0)
+        pair(0, c, 0, core).start()
+
+    join(0)
+    open_chunk(0)
+
     @pl.loop(0, chunks + 2)
     def _(i):
         c1, c2 = i - 1, i - 2
 
-        def open_chunk():
-            for d in range(2):
-                ring_send(d, i, 0)
-            pair(0, i, 0, core).start()
-
-        @pl.when((i < chunks) & (i != 1))
-        def _():
-            open_chunk()
-
         @pl.when((c1 >= 0) & (c1 < chunks))
         def _():
             arrived(c1, 1)
 
-        @pl.when(i == 1)
-        def _():
-            open_chunk()
+        @pl.when(i + 1 < chunks)
+        def _():
+            join(i + 1)
 
         @pl.when(i == 2)
         def _():
@@ -360,14 +358,15 @@
 
         @pl.when(i + 1 < chunks)
         def _():
-            join(i + 1)
+            open_chunk(i + 1)
 
         @pl.when(c2 >= 0)
         def _():
             compute(c2, SUB // 2)
             collect(c2, send, half)
             collect(c2, mine_ref, 0)
-            slab_copy(c2).start()
+            for q in range(half // TILE):
+                slab_copy(c2, q).start()
 
     @pl.loop(0, chunks)
     def _(c):
@@ -383,30 +382,32 @@
 
         for_far(c, act)
         swap(c).wait_send()
-        slab_copy(c).wait_send()
-        slab_copy(c).wait_recv()
-
-
-def last_kernel(rotations, length, wide, mz_ref, mine_ref, far_ref, out_ref, hold):
-    mz = mz_ref[...]
-
-    @pl.loop(0, wide, unroll=2)
-    def _(x):
-        cols = []
-        for r in range(rotations):
-            tiles = []
-            for ref in (mine_ref, far_ref):
-                tiles += [ref[t, r, x] for t in range(ref.shape[0])]
-            cols.append(jnp.concatenate(tiles, 0))
-        scores = dot(mz, jnp.concatenate(cols, 1))
-        best = scores[:, :length]
-        for r in range(1, rotations):
-            best = jnp.maximum(best, scores[:, r * length : (r + 1) * length])
-        hold[pl.ds(x * length, length), :] = best
-
-    @pl.loop(0, length, unroll=4)
-    def _(z):
-        out_ref[z] = hold[pl.ds(z, wide, stride=length), :].astype(bf16)
+
+    @pl.loop(0, half // TILE)
+    def _(q):
+        @pl.loop(0, chunks)
+        def _(c):
+            slab_copy(c, q).wait_send()
+            slab_copy(c, q).wait_recv()
+
+        @pl.loop(0, TILE, unroll=2)
+        def _(x):
+            cols = []
+            for r in range(rotations):
+                tiles = [
+                    ref[t, r, q * TILE + x] for ref in (mine_ref, far_ref) for t in range(chunks)
+                ]
+                cols.append(jnp.concatenate(tiles, 0))
+            scores = dot(mz_ref[...], jnp.concatenate(cols, 1))
+            best = scores[:, :length]
+            for r in range(1, rotations):
+                best = jnp.maximum(best, scores[:, r * length : (r + 1) * length])
+            hold[0, pl.ds(x * length, length), :] = best
+
+        @pl.loop(0, length, unroll=4)
+        def _(z):
+            at = pl.ds(pl.multiple_of(q * TILE, TILE), TILE)
+            out_ref[z, at, :] = hold[0, pl.ds(z, TILE, stride=length), :].astype(bf16)
 
 
 def quick_body(groups, ligand_grids, receptor_kernel):
@@ -445,12 +446,14 @@
     hops = groups // 4
     part = jax.ShapeDtypeStruct((chunks, rotations, half, TILE, length), bf16)
     dma = pltpu.SemaphoreType.DMA
-    keep, far = pl.pallas_call(
+    best = pl.pallas_call(
         functools.partial(score_kernel, rotations, groups, length, chunks),
-        out_shape=[part, part],
-        in_specs=[whole] * 3 + [pl.BlockSpec(memory_space=pl.ANY), whole, whole],
-        out_specs=[whole] * 2,
+        out_shape=jax.ShapeDtypeStruct((length, half, length), bf16),
+        in_specs=[whole] * 4 + [pl.BlockSpec(memory_space=pl.ANY), whole, whole],
+        out_specs=whole,
         scratch_shapes=[
+            pltpu.VMEM(part.shape, bf16),
+            pltpu.VMEM(part.shape, bf16),
             pltpu.VMEM((groups, half, grids, TILE, length), bf16),
             pltpu.VMEM(other.shape, bf16),
             pltpu.VMEM(rec.shape, bf16),
@@ -463,24 +466,14 @@
             dma((2, chunks, hops)),
             dma((2, chunks, hops + 1)),
             dma((2, chunks, hops + 1)),
-            dma((chunks,)),
-            dma((chunks,)),
+            dma((chunks, half // TILE)),
+            dma((chunks, half // TILE)),
         ],
         compiler_params=pltpu.CompilerParams(
             collective_id=0, has_side_effects=True, vmem_limit_bytes=60 * 2**20
         ),
-    )(fx, ix, iy, rec, mine, other)
-
-    wide = TILE
-    best = pl.pallas_call(
-        functools.partial(last_kernel, rotations, length, wide),
-        grid=(half // wide,),
-        out_shape=jax.ShapeDtypeStruct((length, half, length), bf16),
-        in_specs=[pl.BlockSpec((length, side), lambda t: (0, 0))]
-        + [pl.BlockSpec((chunks, rotations, wide, TILE, length), lambda t: (0, 0, t, 0, 0))] * 2,
-        out_specs=pl.BlockSpec((length, wide, length), lambda t: (0, t, 0)),
-        scratch_shapes=[pltpu.VMEM((wide * length, length), f32)],
-    )(mz, keep, far)
+    )(fx, ix, iy, mz, rec, mine, other)
+
     return best[None]
 
 
@@ -496,6 +489,7 @@
         and length % 128 == 0
         and (length // 2) % SUB == 0
         and groups == 4 * 4
+        and (length // 2) % TILE == 0
     )
     if fits:
         return quick_body(groups, ligand_grids, receptor_kernel)

time: 194 us -> 183 us (0.943)
  Pallas kernels: 163 us -> 149 us
  local copies, waits for them, and re-layouts: 3.01 us -> 6.11 us
    pallas_call x1 -> x0, Pallas kernels: 11.8 us -> none  [quick_body(): pl.pallas_call(functools.partial(last_kernel, rotations, length, wide), g...]
    unnamed x10 -> x11, local copies, waits for them, and re-layouts: 0.98 us -> 4.06 us
    pallas_call x1, Pallas kernels: 140 us -> 138 us  [quick_body(): pl.pallas_call(functools.partial(score_kernel, rotations, groups, length,...]
where the time goes in v4:
time: 183 us
  Pallas kernels  149 us (81%)
  waiting for transfers between devices  20.8 us (11%)
  starting transfers between devices  7.4 us (4%)
  local copies, waits for them, and re-layouts  6.11 us (3%)
    pallas_call x1, Pallas kernels, quick_body(): pl.pallas_call(functools.partial(score_kernel, rotations, groups, length,...  138 us
    all_to_all x1, waiting for transfers between devices, quick_body(): lax.all_to_all(blocks, 'grp', split_axis=0, concat_axis=0, tiled=True)  20.8 us
    all_to_all x1, starting transfers between devices, quick_body(): lax.all_to_all(blocks, 'grp', split_axis=0, concat_axis=0, tiled=True)  7.4 us
    pallas_call x1, Pallas kernels, quick_body(): pl.pallas_call(functools.partial(zy_kernel, rotations, groups, block, len...  6.03 us
    pallas_call x1, Pallas kernels, quick_body(): pl.pallas_call(functools.partial(split_kernel, rotations, pairs, depth, w...  5.09 us
    unnamed x11, local copies, waits for them, and re-layouts  4.06 us
  transfers between devices with their start and end apart: 1, of which 1 were waited for; matrix products, arithmetic and copies ran while one was open for 1% of the time, Pallas kernels for 0%

profile of v4, /device:TPU:0, one launch (start us, length us, event | category | flops | bytes accessed | tf_op | source)
XLA Modules:
  0.0 183.0 jit_solution(3098156064280923621)
XLA Ops:
  0.0 0.0 copy-start.4
  0.0 0.0 copy-start.3
  0.0 0.0 copy-start.1
  0.0 0.0 copy-start.2
  0.0 5.1 %shard_map.82 = bf16[16,4,4,16,128]{4,3,2,1,0:T(8,128)(2,1)} custom-call(f32[4096,128]{1,0:T(8,128)} %bitcast.13), custom_call_target="tpu_custom_call" | custom-call | tf_op jit(solution)/shard_map/pallas_call | solution.py:428
  5.1 7.4 %all-to-all-start = ((bf16[16,4,4,16,128]{4,3,2,1,0:T(8,128)(2,1)}), bf16[16,4,4,16,128]{4,3,2,1,0:T(8,128)(2,1)S(1)}, u32[]{:S(2)}, u32[]{:S(2)}) async-start(bf16[16,4,4,16,128]{4,3,2,1,0:T(8,128)(2,1)} %shard_map.82), calls=%async_computation | async-start | bytes 2097152 | tf_op jit(solution)/shard_map/all_to_all | solution.py:434
  12.5 0.0 copy-done.4
  12.5 0.6 dynamic-slice_bitcast_fusion.3.mz_ref
  13.2 0.0 copy-done.3
  13.2 0.7 dynamic-slice_bitcast_fusion.2.fx_ref
  13.8 0.0 copy-done.1
  13.8 0.0 copy-done.2
  13.8 0.7 dynamic-slice_bitcast_fusion
  14.6 20.8 %all-to-all-done.in_ref = bf16[16,4,4,16,128]{4,3,2,1,0:T(8,128)(2,1)S(1)} async-done(((bf16[16,4,4,16,128]{4,3,2,1,0:T(8,128)(2,1)}), bf16[16,4,4,16,128]{4,3,2,1,0:T(8,128)(2,1)S(1)}, u32[]{:S(2)}, u32[]{:S(2)}) %all-to-all-start) | async-done | bytes 1048608 | tf_op jit(solution)/shard_map/all_to_all | solution.py:434
  35.4 0.0 copy-start
  35.4 1.0 copy-done
  36.4 6.0 %shard_map.83 = (bf16[64,4,8,128]{3,2,1,0:T(8,128)(2,1)}, bf16[64,4,8,128]{3,2,1,0:T(8,128)(2,1)}) custom-call(bf16[256,256]{1,0:T(8,128)(2,1)} %get-tuple-element.9.fz_ref, bf16[256,256]{1,0:T(8,128)(2,1)} %constant.43.fy_ref, bf16[16,4,4,16,128]{4,3,2,1,0:T(8,128)(2,1)} %copy-done), custom_call_target="tpu_custom_call" | custom-call | tf_op jit(solution)/shard_map/pallas_call | solution.py:436
  42.4 137.5 %shard_map.84 = bf16[128,64,128]{2,1,0:T(8,128)(2,1)} custom-call(bf16[256,256]{1,0:T(8,128)(2,1)} %dynamic-slice_bitcast_fusion.2.fx_ref, bf16[256,256]{1,0:T(8,128)(2,1)} %get-tuple-element.10.ix_ref, bf16[256,256]{1,0:T(8,128)(2,1)} %constant.40.iy_ref, bf16[128,256]{1,0:T(8,128)(2,1)} %dynamic-slice_bitcast_fusion.3.mz_ref, ...), custom_call_target="tpu_custom_call" | custom-call | tf_op jit(solution)/shard_map/pallas_call | solution.py:449
  179.9 3.1 %copy.10 = bf16[1,128,64,128]{3,2,1,0:T(8,128)(2,1)} copy(bf16[1,128,64,128]{3,2,1,0:T(8,128)(2,1)} %bitcast.12) | data formatting | bytes 4194304
Async XLA Ops:
  0.0 12.5 %copy-start.4 = (bf16[2,128,256]{2,1,0:T(8,128)(2,1)S(1)}, bf16[2,128,256]{2,1,0:T(8,128)(2,1)}, u32[]{:S(2)}) copy-start(bf16[2,128,256]{2,1,0:T(8,128)(2,1)} %constant.41) | copy-start | bytes 393220
  0.0 13.2 %copy-start.3 = (bf16[2,256,256]{2,1,0:T(8,128)(2,1)S(1)}, bf16[2,256,256]{2,1,0:T(8,128)(2,1)}, u32[]{:S(2)}) copy-start(bf16[2,256,256]{2,1,0:T(8,128)(2,1)} %constant.38) | copy-start | bytes 786436
  0.0 13.8 %copy-start.1 = (bf16[2,256,256]{2,1,0:T(8,128)(2,1)S(1)}, bf16[2,256,256]{2,1,0:T(8,128)(2,1)}, u32[]{:S(2)}) copy-start(bf16[2,256,256]{2,1,0:T(8,128)(2,1)} %constant.42) | copy-start | bytes 786436
  0.0 13.8 %copy-start.2 = (bf16[2,256,256]{2,1,0:T(8,128)(2,1)S(1)}, bf16[2,256,256]{2,1,0:T(8,128)(2,1)}, u32[]{:S(2)}) copy-start(bf16[2,256,256]{2,1,0:T(8,128)(2,1)} %constant.39) | copy-start | bytes 786436
  5.1 30.3 %all-to-all-start = ((bf16[16,4,4,16,128]{4,3,2,1,0:T(8,128)(2,1)}), bf16[16,4,4,16,128]{4,3,2,1,0:T(8,128)(2,1)S(1)}, u32[]{:S(2)}, u32[]{:S(2)}) async-start(bf16[16,4,4,16,128]{4,3,2,1,0:T(8,128)(2,1)} %shard_map.82), calls=%async_computation | async-start | bytes 2097152 | tf_op jit(solution)/shard_map/all_to_all | solution.py:434
  35.4 1.0 copy-start
